TPU v7x, 32 devices: a whole 2x2x4 slice. The times are simulated.
32 devices in a mesh: parts: 2 (over x), tile: 16 (over z, y, core).
Axes of the slice: x: 2, y: 2, z: 4, core: 2. Of those that a mesh axis runs over, the one named last changes fastest.
Arguments:
- images: bfloat16 [8, 4096, 256], P('parts', 'tile'), parts along dimension 0, may hold values from -6 to 6
- section_order: int32 [6], P('parts'), parts along dimension 0, may hold values from 0 to 2, each once
- prev_field: float32 [4, 2048, 128], P('parts', 'tile'), parts along dimension 0, may hold values from -8 to 8
- conv1_weight: bfloat16 [32, 9], replicated, may hold values from -2 to 2
- conv1_bias: float32 [32], replicated, may hold values from -3 to 3
- conv2_weight: bfloat16 [9, 32, 32], replicated, may hold values from -0.375 to 0.375
- conv2_bias: float32 [32], replicated, may hold values from -3 to 3
Outputs:
- fields: float32 [6, 2, 2048, 128], P('parts', None, 'tile'), parts along dimension 0
There are 2 independent parts, one for each index of `parts`. A program takes and returns all parts, laid end to end along the dimension named above; an argument that names none is the same for every part. Nothing has to cross between parts.
Inputs may be any that keep to these rules, and one draw needn't show every extreme that they name: section_order is a permutation of 0 .. 2.
All inputs are finite; a program needn't handle non-finite values.
Results may differ from a plain program's by a relative error of at most 0.0043.
Values may be sent and summed in bfloat16 or wider, within the bound.
No kernel may reach another device: no remote copies, remote signals or barrier semaphores. Data moves between devices by JAX's collectives and lax.ppermute only.
A program may use at most 64 MiB of HBM per device.

v0:
```python
import functools
import math

import jax
import jax.numpy as jnp
import numpy as np
from jax import lax
from jax.experimental import pallas as pl
from jax.experimental.pallas import tpu as pltpu
from jax.sharding import PartitionSpec as P

SHARPNESS = 16.0
REACH = 4
LANES = 128
WIDE = 256
HALO = 32
FIELD_HALO = 16
PITCH = 40
BIAS_LANE = 248
PAD = 8
WINDOWS = 8


def first_layer_selector():
    table = np.zeros((WINDOWS, WIDE, 8 * 9 + 3), np.float32)
    for window in range(WINDOWS):
        for row in range(2):
            for pixel in range(4):
                for row_tap in range(3):
                    for col_tap in range(3):
                        pixel_row = 2 * row + row_tap
                        column = 4 * window + 2 * pixel + col_tap
                        lane = PITCH * pixel_row if pixel_row < 3 else LANES + PITCH * (pixel_row - 3)
                        table[window, lane + column, 9 * (4 * row + pixel) + 3 * row_tap + col_tap] = 1
        for piece in range(3):
            table[window, BIAS_LANE + piece, 72 + piece] = 1
    return table.reshape(WINDOWS * WIDE, -1)


def second_layer_selector():
    table = np.zeros((8, 8, 9), np.float32)
    for row_in in range(2):
        for pixel_in in range(4):
            for slot, row_out in enumerate((2, -1, 0, 1)):
                for pixel_out in range(2):
                    row_step, col_step = row_in - row_out, pixel_in - 1 - pixel_out
                    if abs(row_step) <= 1 and abs(col_step) <= 1:
                        table[4 * row_in + pixel_in, 2 * slot + pixel_out, 3 * (row_step + 1) + col_step + 1] = 1
    return table


def lane_index(shape):
    return lax.broadcasted_iota(jnp.int32, shape, len(shape) - 1)


def kernel(
    sections, rows, total_rows, channels,
    meta_ref, img_ref, lo_ref, hi_ref, fld_ref, flo_ref, fhi_ref, w1_ref, w2_ref, b2_ref,
    out_ref, z_ref, x_ref, a_ref, o_ref, t_ref, f_ref,
):
    groups = a_ref.shape[0]
    span = x_ref.shape[0] // groups
    per = LANES // channels
    lane = lane_index((1, LANES))
    slot = lane // channels
    tile = meta_ref[0]
    pairs_total = total_rows // 2

    z_ref[...] = jnp.zeros_like(z_ref)
    f_ref[0, :, 0:FIELD_HALO, :] = flo_ref[...]
    f_ref[0, :, FIELD_HALO : FIELD_HALO + rows, :] = fld_ref[...]
    f_ref[0, :, FIELD_HALO + rows : 2 * FIELD_HALO + rows, :] = fhi_ref[...]

    def encode(k, carry):
        extra = REACH * (sections - k)
        section = jnp.where(k == 0, 0, 1 + meta_ref[jnp.maximum(k, 1)])
        base = pl.multiple_of(2 * extra, 8)
        for half in range(2):
            cols = slice(LANES * half, LANES * (half + 1))
            z_ref[half, pl.ds(base, HALO), :] = lo_ref[section, :, cols].astype(jnp.float32)
            z_ref[half, pl.ds(base + HALO, 2 * rows), :] = img_ref[section, :, cols].astype(jnp.float32)
            z_ref[half, pl.ds(base + HALO + 2 * rows, HALO), :] = hi_ref[section, :, cols].astype(jnp.float32)
        pair = lax.broadcasted_iota(jnp.int32, (span, LANES), 0) + tile * (rows // 2) - 1 - extra // 2
        valid = jnp.where((pair >= 0) & (pair < pairs_total), 1.0, 0.0)

        for group in range(groups):
            side, place = divmod(group, groups // 2)
            pieces = []
            for row in range(5):
                here = z_ref[side, pl.ds(HALO - 5 + row, span, stride=4), :]
                if place == 0 or (place == groups // 2 - 1 and side == 0):
                    if side == 0 and place == 0:
                        here = jnp.where(lane < LANES // 2, here, 0.0)
                    else:
                        other = z_ref[1 - side, pl.ds(HALO - 5 + row, span, stride=4), :]
                        low, high = (here, other) if side == 1 else (other, here)
                        here = jnp.where(lane < LANES // 2, low, high)
                start = PITCH * (row % 3)
                shift = (start - (2 * LANES // groups * place - 3)) % LANES
                pieces.append(pltpu.roll(here, shift, 1))
            left = jnp.where(lane < PITCH, pieces[0], jnp.where(lane < 2 * PITCH, pieces[1], pieces[2]))
            right = jnp.where(lane < PITCH, pieces[3], jnp.where(lane < BIAS_LANE - LANES, pieces[4], valid))
            x_ref[pl.ds(span * group, span), 0:LANES] = (left * valid).astype(jnp.bfloat16)
            x_ref[pl.ds(span * group, span), LANES:WIDE] = (right * valid).astype(jnp.bfloat16)

        def column(xh, carry):
            for part in range(2):
                window = xh + 4 * part
                first = jnp.dot(x_ref[...], w1_ref[window], preferred_element_type=jnp.float32)
                first = jnp.maximum(first, 0.0).reshape(groups, span, WIDE)
                edge = (lane_index((1, 1, WIDE)) // channels) % 4
                group_at = lax.broadcasted_iota(jnp.int32, (groups, 1, WIDE), 0)
                if part == 0:
                    drop = (edge == 0) & (group_at == 0) & (xh == 0)
                else:
                    drop = (edge == 3) & (group_at == groups - 1) & (xh == 3)
                first = jnp.where(drop, 0.0, first)
                first = first.reshape(groups * span, WIDE).astype(jnp.bfloat16)
                second = jnp.dot(first, w2_ref[...], preferred_element_type=jnp.float32)
                second = second.reshape(groups, span, WIDE)
                a_ref[:, PAD : PAD + span, :] = second[:, :, 0:LANES]
                for group in range(groups):
                    above = a_ref[group, PAD - 1 : PAD - 1 + span, :]
                    below = a_ref[group, PAD + 1 : PAD + 1 + span, :]
                    summed = second[group, :, LANES:WIDE] + jnp.where(lane < LANES // 2, above, below)
                    o_ref[part, group] = jnp.tanh(summed + b2_ref[...]) * valid
            for side in range(2):
                for half in range(2):
                    at = 4 * side + 2 * half
                    s0, s1, s2, s3 = o_ref[0, at], o_ref[1, at], o_ref[0, at + 1], o_ref[1, at + 1]
                    low = lane < LANES // 2
                    even = slot % 2 == 0
                    a0, a2 = jnp.where(low, s0, pltpu.roll(s2, 64, 1)), jnp.where(low, pltpu.roll(s0, 64, 1), s2)
                    a1, a3 = jnp.where(low, s1, pltpu.roll(s3, 64, 1)), jnp.where(low, pltpu.roll(s1, 64, 1), s3)
                    back = LANES - channels
                    c0, c1 = jnp.where(even, a0, pltpu.roll(a1, channels, 1)), jnp.where(even, pltpu.roll(a0, back, 1), a1)
                    c2, c3 = jnp.where(even, a2, pltpu.roll(a3, channels, 1)), jnp.where(even, pltpu.roll(a2, back, 1), a3)
                    for parity, pixel, value in ((0, 0, c0), (0, 1, c1), (1, 0, c2), (1, 1, c3)):
                        t_ref[k, 4 + 2 * xh + pixel, parity, side, half, PAD : PAD + span, :] = value
            return carry

        lax.fori_loop(0, 4, column, 0)

        def surround(at, carry):
            x_low, parity = at // 2, at % 2
            rows_at = slice(PAD, PAD + span)
            order = [(0, 0), (0, 1), (1, 0), (1, 1)]
            left = [pltpu.roll(t_ref[k, 8 + x_low, parity, s, h, rows_at, :], channels, 1) for s, h in order]
            right = [pltpu.roll(t_ref[k, 4 + x_low, parity, s, h, rows_at, :], LANES - channels, 1) for s, h in order]
            for n, (s, h) in enumerate(order):
                before = left[n - 1] if n else jnp.zeros_like(left[0])
                after = right[n + 1] if n < 3 else jnp.zeros_like(right[0])
                t_ref[k, x_low, parity, s, h, rows_at, :] = jnp.where(slot == 0, before, left[n])
                t_ref[k, 12 + x_low, parity, s, h, rows_at, :] = jnp.where(slot == per - 1, after, right[n])
            return carry

        @pl.when(k < sections)
        def _():
            lax.fori_loop(0, 8, surround, 0)

        return carry

    lax.fori_loop(0, sections + 1, encode, 0)

    scale = SHARPNESS / channels * math.log2(math.e)
    sub8 = lax.broadcasted_iota(jnp.int32, (8, LANES), 0)
    lane8 = lane_index((8, LANES))
    wide = lane_index((1, WIDE))
    x_of = (wide // 8) % 4
    y_of = 2 * (wide % 4) + (wide // 4) % 2
    row_at = 2 * lax.broadcasted_iota(jnp.int32, (2, 8, WIDE), 1) + lax.broadcasted_iota(jnp.int32, (2, 8, WIDE), 0)
    row_weight = row_at.astype(jnp.float32)
    row_mask = jnp.where((row_at >= y_of) & (row_at <= y_of + 2 * REACH), 1.0, 0.0)
    pick = channels * ((lane8 // 8) % 4) + 8 * (lane8 % 4) + 4 * (sub8 % 2) + sub8 // 2
    patch = [jnp.where(slot == q, 1.0, 0.0).astype(jnp.bfloat16) for q in range(per)]

    def gather(values, index):
        return jnp.take_along_axis(values, index, axis=1, mode="promise_in_bounds")

    def block(k, i):
        extra = REACH * (sections - k)
        down = jnp.zeros((8, LANES), jnp.float32)
        across = jnp.zeros((8, LANES), jnp.float32)
        for side in range(2):
            for h in range(2):
                lhs, rhs = [], []
                for half in range(2):
                    window = t_ref[k - 1, 4 * h : 4 * h + 12, :, side, half, pl.ds(PAD + 1 + 4 * i, 8), :]
                    lhs.append(window.reshape(12 * 16, LANES).astype(jnp.bfloat16))
                    even = t_ref[k, 4 + 4 * h : 8 + 4 * h, 0, side, half, pl.ds(PAD + 1 + 4 * i, 8), :]
                    odd = t_ref[k, 4 + 4 * h : 8 + 4 * h, 1, side, half, pl.ds(PAD - 3 + 4 * i, 8), :]
                    current = jnp.where(sub8 < 4, even, odd) * scale
                    current = current.reshape(32, LANES).astype(jnp.bfloat16)
                    nothing = jnp.zeros_like(current)
                    for q in range(per):
                        masked = current * patch[q]
                        rhs.append(jnp.concatenate([masked, nothing] if half == 0 else [nothing, masked], axis=1))
                lhs = jnp.concatenate(lhs, axis=1)
                rhs = jnp.concatenate(rhs, axis=0)
                score = lax.dot_general(lhs, rhs, (((1,), (1,)), ((), ())), preferred_element_type=jnp.float32)
                weight = jnp.exp2(score).reshape(12, 2, 8, WIDE)
                running = jnp.zeros((2, 8, WIDE), jnp.float32)
                moment = jnp.zeros((2, 8, WIDE), jnp.float32)
                for u in range(11, -1, -1):
                    term = weight[u]
                    if u < 3:
                        term = jnp.where(x_of <= u, term, 0.0)
                    if u > 8:
                        term = jnp.where(x_of >= u - 8, term, 0.0)
                    running = running + term
                    if u:
                        moment = moment + running
                running = running * row_mask
                moment = moment * row_mask
                total = jnp.sum(running[0] + running[1], axis=0, keepdims=True)
                moved = running * row_weight
                y_sum = jnp.sum(moved[0] + moved[1], axis=0, keepdims=True)
                x_sum = jnp.sum(moment[0] + moment[1], axis=0, keepdims=True)
                y_mean, x_mean = y_sum / total, x_sum / total
                for half in range(2):
                    keep = (lane8 // 64 == side) & ((lane8 // 32) % 2 == half) & ((lane8 // 4) % 2 == h)
                    cols = slice(LANES * half, LANES * (half + 1))
                    down = jnp.where(keep, gather(jnp.broadcast_to(y_mean[:, cols], (8, LANES)), pick), down)
                    across = jnp.where(keep, gather(jnp.broadcast_to(x_mean[:, cols], (8, LANES)), pick), across)
        down = down - (REACH + sub8).astype(jnp.float32)
        across = across - (REACH + lane8 % 4).astype(jnp.float32)

        whole = jnp.floor(across)
        part = across - whole
        left = lane8 + whole.astype(jnp.int32)
        right = left + 1
        left_weight = jnp.where((left >= 0) & (left < LANES), 1.0 - part, 0.0)
        right_weight = jnp.where((right >= 0) & (right < LANES), part, 0.0)
        left = jnp.clip(left, 0, LANES - 1)
        right = jnp.clip(right, 0, LANES - 1)
        sums = [down, across]
        shift = jnp.where(k == 1, FIELD_HALO - REACH * sections, 0)
        for step in range(-REACH, REACH + 1):
            row_part = jnp.maximum(0.0, 1.0 - jnp.abs(down - step))
            for c in range(2):
                values = f_ref[k - 1, c, pl.ds(8 * i + REACH + step + shift, 8), :]
                mixed = left_weight * gather(values, left) + right_weight * gather(values, right)
                sums[c] = sums[c] + row_part * mixed
        row = sub8 + 8 * i - extra + tile * rows
        inside = (row >= 0) & (row < total_rows)
        for c in range(2):
            f_ref[k, c, pl.ds(pl.multiple_of(8 * i, 8), 8), :] = jnp.where(inside, sums[c], 0.0)

    def advance(k, carry):
        def step(i, carry):
            block(k, i)
            return carry

        lax.fori_loop(0, (rows + 2 * REACH * (sections - k)) // 8, step, 0)
        return carry

    lax.fori_loop(1, sections + 1, advance, 0)
    for k in range(1, sections + 1):
        extra = REACH * (sections - k)
        out_ref[k - 1] = f_ref[k, :, extra : extra + rows, :]


def on_device(images, section_order, prev_field, conv1_weight, conv1_bias, conv2_weight, conv2_bias):
    count = lax.axis_size("tile")
    forward = [(i, i + 1) for i in range(count - 1)]
    backward = [(target, source) for source, target in forward]
    pixel_rows, columns = images.shape[1:]
    sections = section_order.shape[0]
    rows = prev_field.shape[1]
    channels = conv1_weight.shape[0]
    lo = lax.ppermute(images[:, pixel_rows - HALO :], "tile", forward)
    hi = lax.ppermute(images[:, :HALO], "tile", backward)
    flo = lax.ppermute(prev_field[:, rows - FIELD_HALO :], "tile", forward)
    fhi = lax.ppermute(prev_field[:, :FIELD_HALO], "tile", backward)

    slots = WIDE // channels
    taps = jnp.kron(jnp.eye(slots, dtype=jnp.float32), conv1_weight.astype(jnp.float32).T)
    rest = jnp.tile(conv1_bias, slots)
    rounded = []
    for _ in range(3):
        top = lax.reduce_precision(rest, 8, 7)
        rounded.append(top)
        rest = rest - top
    taps = jnp.concatenate([taps, jnp.stack(rounded)], axis=0).astype(jnp.bfloat16)
    w1 = jnp.dot(jnp.asarray(first_layer_selector(), jnp.bfloat16), taps, preferred_element_type=jnp.float32)
    w1 = w1.astype(jnp.bfloat16).reshape(WINDOWS, WIDE, WIDE)
    w2 = jnp.einsum(
        "bdt,toc->bcdo", jnp.asarray(second_layer_selector(), jnp.bfloat16), conv2_weight,
        preferred_element_type=jnp.float32,
    ).astype(jnp.bfloat16).reshape(WIDE, WIDE)
    b2 = jnp.tile(conv2_bias, LANES // channels)[None]
    meta = jnp.concatenate([lax.axis_index("tile").astype(jnp.int32)[None], section_order])

    groups = columns // (4 * WINDOWS)
    span = (rows + 2 * REACH * sections) // 2 + 4
    vmem = pl.BlockSpec(memory_space=pltpu.VMEM)
    return pl.pallas_call(
        functools.partial(kernel, sections, rows, rows * count, channels),
        out_shape=jax.ShapeDtypeStruct((sections, 2, rows, prev_field.shape[2]), jnp.float32),
        in_specs=[pl.BlockSpec(memory_space=pltpu.SMEM)] + [vmem] * 9,
        out_specs=vmem,
        scratch_shapes=[
            pltpu.VMEM((2, 2 * rows + 96, LANES), jnp.float32),
            pltpu.VMEM((groups * span, WIDE), jnp.bfloat16),
            pltpu.VMEM((groups, span + 2 * PAD, LANES), jnp.float32),
            pltpu.VMEM((2, groups, span, LANES), jnp.float32),
            pltpu.VMEM((sections + 1, 16, 2, 2, 2, span + 2 * PAD, LANES), jnp.float32),
            pltpu.VMEM((sections + 1, 2, rows + 2 * FIELD_HALO + 8, LANES), jnp.float32),
        ],
        compiler_params=pltpu.CompilerParams(vmem_limit_bytes=60 * 1024 * 1024),
        name="align",
    )(meta, images, lo, hi, prev_field, flo, fhi, w1, w2, b2)


def solution(mesh):
    in_specs = (P("parts", "tile", None), P("parts"), P("parts", "tile", None), P(), P(), P(), P())
    out_specs = P("parts", None, "tile", None)
    return jax.shard_map(on_device, mesh=mesh, in_specs=in_specs, out_specs=out_specs, check_vma=False)
```

profile of v0, /device:TPU:21, one launch (start us, length us, event | category | flops | bytes accessed | tf_op | source)
XLA Modules:
  0.0 75.7 jit_solution(10781782043818936107)
XLA Ops:
  0.0 0.0 copy-start.9
  0.0 0.9 %fusion.13 = (bf16[4,32,256]{2,1,0:T(8,128)(2,1)S(1)}, bf16[4,32,256]{2,1,0:T(8,128)(2,1)S(1)}) fusion(bf16[4,256,256]{2,1,0:T(8,128)(2,1)} %img_ref.1), kind=kLoop, calls=%fused_computation.23 | loop fusion | bytes 262144 | tf_op jit(solution)/shard_map/slice | solution.py:272
  1.0 3.7 %collective-permute-start = (bf16[4,32,256]{2,1,0:T(8,128)(2,1)S(1)}, bf16[4,32,256]{2,1,0:T(8,128)(2,1)S(1)}, u32[]{:S(2)}, u32[]{:S(2)}) collective-permute-start(bf16[4,32,256]{2,1,0:T(8,128)(2,1)S(1)} %get-tuple-element.6), channel_id=1, source_target_pairs={{0,1},{1,2},{2,3},{3,4},{4,5},{5,6},{6,7},{7,8},{8,9},{9,10},{10,1... | collective-permute-start | bytes 196616 | tf_op jit(solution)/shard_map/ppermute | solution.py:271
  4.7 1.9 %collective-permute-start.1 = (bf16[4,32,256]{2,1,0:T(8,128)(2,1)S(1)}, bf16[4,32,256]{2,1,0:T(8,128)(2,1)S(1)}, u32[]{:S(2)}, u32[]{:S(2)}) collective-permute-start(bf16[4,32,256]{2,1,0:T(8,128)(2,1)S(1)} %get-tuple-element.5), channel_id=1, source_target_pairs={{1,0},{2,1},{3,2},{4,3},{5,4},{6,5},{7,6},{8,7},{9,8},{10,9},{11,1... | collective-permute-start | bytes 196616 | tf_op jit(solution)/shard_map/ppermute | solution.py:272
  6.6 0.7 fusion.14
  7.4 4.5 %collective-permute-start.2 = (f32[2,16,128]{2,1,0:T(8,128)S(1)}, f32[2,16,128]{2,1,0:T(8,128)S(1)}, u32[]{:S(2)}, u32[]{:S(2)}) collective-permute-start(f32[2,16,128]{2,1,0:T(8,128)S(1)} %get-tuple-element.8), channel_id=1, source_target_pairs={{0,1},{1,2},{2,3},{3,4},{4,5},{5,6},{6,7},{7,8},{8,9},{9,10},{10,1... | collective-permute-start | bytes 49160 | tf_op jit(solution)/shard_map/ppermute | solution.py:273
  11.9 1.9 %collective-permute-start.3 = (f32[2,16,128]{2,1,0:T(8,128)S(1)}, f32[2,16,128]{2,1,0:T(8,128)S(1)}, u32[]{:S(2)}, u32[]{:S(2)}) collective-permute-start(f32[2,16,128]{2,1,0:T(8,128)S(1)} %get-tuple-element.7), channel_id=1, source_target_pairs={{1,0},{2,1},{3,2},{4,3},{5,4},{6,5},{7,6},{8,7},{9,8},{10,9},{11,1... | collective-permute-start | bytes 49160 | tf_op jit(solution)/shard_map/ppermute | solution.py:274
  13.8 0.7 tile.6
  14.5 0.1 tile.7
  14.6 0.7 convert_bitcast_fusion
  15.3 0.1 multiply_convert_fusion
  15.4 0.1 mul.27
  15.5 1.2 %fusion.4 = bf16[8,32,8,32]{1,2,3,0:T(8,128)(2,1)S(1)} fusion(bf16[8,8,9,1]{2,1,3,0:T(8,128)(2,1)} %constant.21, bf16[9,32,32]{2,1,0:T(8,128)(2,1)} %param.14), kind=kOutput, calls=%fused_computation.6 | convolution fusion | flops 1245184 | bytes 150656 | tf_op jit(solution)/shard_map/bdt,toc->bcdo/dot_general | solution.py:287
  16.7 0.0 copy-done.6
  16.7 0.0 copy-done.7
  16.7 0.0 copy-done.8
  16.7 0.0 copy-start.5
  16.8 0.7 fusion.3
  17.5 0.7 pad_add_fusion.meta_ref
  18.1 1.3 %copy.10 = bf16[2048,256]{1,0:T(8,128)(2,1)} copy(bf16[2048,256]{0,1:T(8,128)(2,1)S(1)} %fusion.3) | data formatting | bytes 2097152 | tf_op jit(solution)/shard_map/convert_element_type | solution.py:286
  19.4 0.5 copy.12
  19.9 1.0 %reshape.63.w2_ref = bf16[256,256]{1,0:T(8,128)(2,1)} reshape(bf16[8,32,8,32]{3,2,1,0:T(8,128)(2,1)S(1)} %copy.12) | data formatting | bytes 262144 | tf_op jit(solution)/shard_map/reshape | solution.py:290
  21.0 0.6 broadcast_in_dim_tile.3.b2_ref
  21.5 0.0 collective-permute-done.2.flo_ref
  21.5 0.0 collective-permute-done.3.fhi_ref
  21.5 0.0 collective-permute-done.lo_ref
  21.6 0.0 collective-permute-done.1.hi_ref
  21.6 0.5 copy-done.2
  22.1 0.0 copy-done.3
  22.1 0.0 copy-done
  22.2 0.0 copy-done.1
  22.2 53.5 %align.1 = f32[3,2,128,128]{3,2,1,0:T(8,128)} custom-call(s32[4]{0:T(128)} %pad_add_fusion.meta_ref, bf16[4,256,256]{2,1,0:T(8,128)(2,1)} %img_ref.1, bf16[4,32,256]{2,1,0:T(8,128)(2,1)} %copy-done, bf16[4,32,256]{2,1,0:T(8,128)(2,1)} %copy-done.1, f32[2,128,128]{2,1,0:T(8,128)} %fld_ref.1, f32[2,16,128]{2,1,0:T(8,128)} %copy-done.2, ...), custom_call_target="tpu_custom_call" | custom-call | tf_op jit(solution)/shard_map/align/pallas_call | solution.py:297
  (14 shorter events, 0.0 us)
Async XLA Ops:
  0.0 16.7 %copy-start.6 = (bf16[2048,72]{1,0:T(8,128)(2,1)S(1)}, bf16[2048,72]{1,0:T(8,128)(2,1)}, u32[]{:S(2)}) copy-start(bf16[2048,72]{1,0:T(8,128)(2,1)} %constant.11) | copy-start | bytes 884740
  0.0 16.7 %copy-start.7 = (f32[2048]{0:T(1024)S(1)}, f32[2048]{0:T(1024)}, u32[]{:S(2)}) copy-start(f32[2048]{0:T(1024)} %constant.14) | copy-start | bytes 24580
  0.0 16.7 %copy-start.8 = (f32[2048]{0:T(1024)S(1)}, f32[2048]{0:T(1024)}, u32[]{:S(2)}) copy-start(f32[2048]{0:T(1024)} %constant.17) | copy-start | bytes 24580
  0.0 16.7 %copy-start.9 = (f32[2048]{0:T(1024)S(1)}, f32[2048]{0:T(1024)}, u32[]{:S(2)}) copy-start(f32[2048]{0:T(1024)} %constant.20) | copy-start | bytes 24580
  1.0 20.6 %collective-permute-start = (bf16[4,32,256]{2,1,0:T(8,128)(2,1)S(1)}, bf16[4,32,256]{2,1,0:T(8,128)(2,1)S(1)}, u32[]{:S(2)}, u32[]{:S(2)}) collective-permute-start(bf16[4,32,256]{2,1,0:T(8,128)(2,1)S(1)} %get-tuple-element.6), channel_id=1, source_target_pairs={{0,1},{1,2},{2,3},{3,4},{4,5},{5,6},{6,7},{7,8},{8,9},{9,10},{10,1... | collective-permute-start | bytes 196616 | tf_op jit(solution)/shard_map/ppermute | solution.py:271
  4.7 16.9 %collective-permute-start.1 = (bf16[4,32,256]{2,1,0:T(8,128)(2,1)S(1)}, bf16[4,32,256]{2,1,0:T(8,128)(2,1)S(1)}, u32[]{:S(2)}, u32[]{:S(2)}) collective-permute-start(bf16[4,32,256]{2,1,0:T(8,128)(2,1)S(1)} %get-tuple-element.5), channel_id=1, source_target_pairs={{1,0},{2,1},{3,2},{4,3},{5,4},{6,5},{7,6},{8,7},{9,8},{10,9},{11,1... | collective-permute-start | bytes 196616 | tf_op jit(solution)/shard_map/ppermute | solution.py:272
  7.4 14.2 %collective-permute-start.2 = (f32[2,16,128]{2,1,0:T(8,128)S(1)}, f32[2,16,128]{2,1,0:T(8,128)S(1)}, u32[]{:S(2)}, u32[]{:S(2)}) collective-permute-start(f32[2,16,128]{2,1,0:T(8,128)S(1)} %get-tuple-element.8), channel_id=1, source_target_pairs={{0,1},{1,2},{2,3},{3,4},{4,5},{5,6},{6,7},{7,8},{8,9},{9,10},{10,1... | collective-permute-start | bytes 49160 | tf_op jit(solution)/shard_map/ppermute | solution.py:273
  11.9 9.6 %collective-permute-start.3 = (f32[2,16,128]{2,1,0:T(8,128)S(1)}, f32[2,16,128]{2,1,0:T(8,128)S(1)}, u32[]{:S(2)}, u32[]{:S(2)}) collective-permute-start(f32[2,16,128]{2,1,0:T(8,128)S(1)} %get-tuple-element.7), channel_id=1, source_target_pairs={{1,0},{2,1},{3,2},{4,3},{5,4},{6,5},{7,6},{8,7},{9,8},{10,9},{11,1... | collective-permute-start | bytes 49160 | tf_op jit(solution)/shard_map/ppermute | solution.py:274
  16.7 0.7 copy-start.5
  19.4 1.5 %copy-start.4 = (f32[32]{0:T(128)S(1)}, f32[32]{0:T(128)}, u32[]{:S(2)}) copy-start(f32[32]{0:T(128)} %param.15) | copy-start | bytes 388
  21.5 0.6 copy-start.2
  21.5 0.6 copy-start.3
  21.6 0.6 copy-start
  21.6 0.6 copy-start.1
where the time goes:
time: 76.9 us; the launch traced here: 75.7 us
  Pallas kernels  53.5 us (70%)
  starting transfers between devices  12.1 us (16%)
  local copies, waits for them, and re-layouts  6.61 us (9%)
  matrix products  1.9 us (2%)
  other arithmetic  1.45 us (2%)
    pallas_call x1, Pallas kernels, on_device(): pl.pallas_call(functools.partial(kernel, sections, rows, rows * count, ch...  53.5 us
    ppermute x1, starting transfers between devices, on_device(): flo = lax.ppermute(prev_field[:, rows - FIELD_HALO:], 'tile', forward)  4.53 us
    ppermute x1, starting transfers between devices, on_device(): lo = lax.ppermute(images[:, pixel_rows - HALO:], 'tile', forward)  3.71 us
    ppermute x1, starting transfers between devices, on_device(): hi = lax.ppermute(images[:, :HALO], 'tile', backward)  1.92 us
    ppermute x1, starting transfers between devices, on_device(): fhi = lax.ppermute(prev_field[:, :FIELD_HALO], 'tile', backward)  1.92 us
  transfers between devices with their start and end apart: 4, of which 0 were waited for; matrix products, arithmetic and copies ran while one was open for 11% of the time, Pallas kernels for 0%

commit v1 on v0

v1 whole, which is shorter than its diff:
```python
import functools
import math

import jax
import jax.numpy as jnp
import numpy as np
from jax import lax
from jax.experimental import pallas as pl
from jax.experimental.pallas import tpu as pltpu
from jax.sharding import PartitionSpec as P

SHARPNESS = 16.0
REACH = 4
LANES = 128
WIDE = 256
HALO = 32
FIELD_HALO = 16
PITCH = 40
BIAS_LANE = 248
PAD = 8
WINDOWS = 8


def first_layer_lanes():
    lanes = np.full((1, LANES), -WIDE, np.int32)
    for slot in range(8):
        for tap in range(9):
            pixel_row = 2 * (slot // 4) + tap // 3
            start = PITCH * pixel_row if pixel_row < 3 else LANES + PITCH * (pixel_row - 3)
            lanes[0, 9 * slot + tap] = start + 2 * (slot % 4) + tap % 3
    return lanes


def prepare(lanes_ref, c1_ref, b1_ref, c2_ref, b2_ref, w1_ref, w2_ref, bias_ref):
    channels, taps = c1_ref.shape

    def indices(shape):
        return [lax.broadcasted_iota(jnp.int32, shape, axis) for axis in range(2)]

    def ones_where(condition):
        return jnp.where(condition, 1.0, 0.0).astype(jnp.bfloat16)

    def repeated(values, dims):
        return lax.dot_general(values, spread, (dims, ((), ())), preferred_element_type=jnp.float32)

    row, col = indices((channels, WIDE))
    spread = ones_where(col % channels == row)

    def pieces(ref):
        rest = jnp.broadcast_to(ref[...], (8, channels))
        row = lax.broadcasted_iota(jnp.int32, (8, channels), 0)
        total = jnp.zeros((8, channels), jnp.float32)
        for n in range(3):
            top = rest.astype(jnp.bfloat16).astype(jnp.float32)
            total = jnp.where(row == n, top, total)
            rest = rest - top
        return repeated(total.astype(jnp.bfloat16), ((1,), (0,)))

    bias_ref[...] = jnp.broadcast_to(jnp.sum(pieces(b2_ref), axis=0, keepdims=True), (8, WIDE))[:, :LANES]

    by_tap = repeated(c1_ref[...], ((0,), (0,)))
    row, col = indices((LANES, WIDE))
    table = jnp.zeros((LANES, WIDE), jnp.float32)
    slot = col // channels
    for tap in range(taps):
        table = jnp.where(row == taps * slot + tap, by_tap[tap : tap + 1], table)
    bias = pieces(b1_ref)
    for n in range(3):
        table = jnp.where(row == 8 * taps + n, bias[n : n + 1], table)
    table = table.astype(jnp.bfloat16)
    row, col = indices((WIDE, LANES))
    bias_lane = (col >= 8 * taps) & (col < 8 * taps + 3) & (row == BIAS_LANE + col - 8 * taps)
    for window in range(WINDOWS):
        pick = ones_where((row == lanes_ref[...] + 4 * window) | bias_lane)
        w1_ref[window] = jnp.dot(pick, table, preferred_element_type=jnp.float32).astype(jnp.bfloat16)

    row, col = indices((WIDE, WIDE))
    slot_in, slot_out = row // channels, col // channels
    row_out = slot_out // 2
    row_out = jnp.where(row_out == 0, 2, row_out - 2)
    row_step = slot_in // 4 - row_out
    col_step = slot_in % 4 - 1 - slot_out % 2
    near = (jnp.abs(row_step) <= 1) & (jnp.abs(col_step) <= 1)
    tap_at = jnp.where(near, 3 * row_step + col_step + 4, -1)
    table = jnp.zeros((WIDE, WIDE), jnp.float32)
    for tap in range(taps):
        block = repeated(c2_ref[tap], ((0,), (0,)))
        table = jnp.where(tap_at == tap, jnp.concatenate([block] * (WIDE // channels), axis=0), table)
    w2_ref[...] = table.astype(jnp.bfloat16)


def lane_index(shape):
    return lax.broadcasted_iota(jnp.int32, shape, len(shape) - 1)


def kernel(
    sections, rows, total_rows, channels,
    order_ref, img_ref, lo_ref, hi_ref, fld_ref, w1_ref, w2_ref, b2_ref,
    out_ref, z_ref, x_ref, a_ref, o_ref, t_ref, f_ref, s_ref,
):
    groups = a_ref.shape[0]
    span = x_ref.shape[0] // groups
    per = LANES // channels
    lane = lane_index((1, LANES))
    slot = lane // channels
    tile = lax.axis_index("tile")
    pairs_total = total_rows // 2

    z_ref[...] = jnp.zeros_like(z_ref)
    pictures = HALO * (sections + 1)
    f_ref[0, :, FIELD_HALO : FIELD_HALO + rows, :] = fld_ref[...]
    for ref, start in ((lo_ref, 0), (hi_ref, FIELD_HALO + rows)):
        for c in range(2):
            both = ref[pictures + FIELD_HALO * c : pictures + FIELD_HALO * (c + 1), :].astype(jnp.float32)
            f_ref[0, c, start : start + FIELD_HALO, :] = both[:, :LANES] + both[:, LANES:]

    def encode(k, carry):
        extra = REACH * (sections - k)
        section = jnp.where(k == 0, 0, 1 + order_ref[jnp.maximum(k - 1, 0)])
        border = pl.ds(pl.multiple_of(HALO * section, HALO), HALO)
        base = pl.multiple_of(2 * extra, 8)
        for half in range(2):
            cols = slice(LANES * half, LANES * (half + 1))
            z_ref[half, pl.ds(base, HALO), :] = lo_ref[border, cols].astype(jnp.float32)
            z_ref[half, pl.ds(base + HALO, 2 * rows), :] = img_ref[section, :, cols].astype(jnp.float32)
            z_ref[half, pl.ds(base + HALO + 2 * rows, HALO), :] = hi_ref[border, cols].astype(jnp.float32)
        pair = lax.broadcasted_iota(jnp.int32, (span, LANES), 0) + tile * (rows // 2) - 1 - extra // 2
        valid = jnp.where((pair >= 0) & (pair < pairs_total), 1.0, 0.0)

        for group in range(groups):
            side, place = divmod(group, groups // 2)
            pieces = []
            for row in range(5):
                here = z_ref[side, pl.ds(HALO - 5 + row, span, stride=4), :]
                if place == 0 or (place == groups // 2 - 1 and side == 0):
                    if side == 0 and place == 0:
                        here = jnp.where(lane < LANES // 2, here, 0.0)
                    else:
                        other = z_ref[1 - side, pl.ds(HALO - 5 + row, span, stride=4), :]
                        low, high = (here, other) if side == 1 else (other, here)
                        here = jnp.where(lane < LANES // 2, low, high)
                start = PITCH * (row % 3)
                shift = (start - (2 * LANES // groups * place - 3)) % LANES
                pieces.append(pltpu.roll(here, shift, 1))
            left = jnp.where(lane < PITCH, pieces[0], jnp.where(lane < 2 * PITCH, pieces[1], pieces[2]))
            right = jnp.where(lane < PITCH, pieces[3], jnp.where(lane < BIAS_LANE - LANES, pieces[4], valid))
            x_ref[pl.ds(span * group, span), 0:LANES] = (left * valid).astype(jnp.bfloat16)
            x_ref[pl.ds(span * group, span), LANES:WIDE] = (right * valid).astype(jnp.bfloat16)

        def column(xh, carry):
            for part in range(2):
                window = xh + 4 * part
                first = jnp.dot(x_ref[...], w1_ref[window], preferred_element_type=jnp.float32)
                first = jnp.maximum(first, 0.0).reshape(groups, span, WIDE)
                edge = (lane_index((1, 1, WIDE)) // channels) % 4
                group_at = lax.broadcasted_iota(jnp.int32, (groups, 1, WIDE), 0)
                if part == 0:
                    drop = (edge == 0) & (group_at == 0) & (xh == 0)
                else:
                    drop = (edge == 3) & (group_at == groups - 1) & (xh == 3)
                first = jnp.where(drop, 0.0, first)
                first = first.reshape(groups * span, WIDE).astype(jnp.bfloat16)
                second = jnp.dot(first, w2_ref[...], preferred_element_type=jnp.float32)
                second = second.reshape(groups, span, WIDE)
                a_ref[:, PAD : PAD + span, :] = second[:, :, 0:LANES]
                for group in range(groups):
                    above = a_ref[group, PAD - 1 : PAD - 1 + span, :]
                    below = a_ref[group, PAD + 1 : PAD + 1 + span, :]
                    summed = second[group, :, LANES:WIDE] + jnp.where(lane < LANES // 2, above, below)
                    o_ref[part, group] = jnp.tanh(summed + b2_ref[0:1, :]) * valid
            for side in range(2):
                for half in range(2):
                    at = 4 * side + 2 * half
                    s0, s1, s2, s3 = o_ref[0, at], o_ref[1, at], o_ref[0, at + 1], o_ref[1, at + 1]
                    low = lane < LANES // 2
                    even = slot % 2 == 0
                    a0, a2 = jnp.where(low, s0, pltpu.roll(s2, 64, 1)), jnp.where(low, pltpu.roll(s0, 64, 1), s2)
                    a1, a3 = jnp.where(low, s1, pltpu.roll(s3, 64, 1)), jnp.where(low, pltpu.roll(s1, 64, 1), s3)
                    back = LANES - channels
                    c0, c1 = jnp.where(even, a0, pltpu.roll(a1, channels, 1)), jnp.where(even, pltpu.roll(a0, back, 1), a1)
                    c2, c3 = jnp.where(even, a2, pltpu.roll(a3, channels, 1)), jnp.where(even, pltpu.roll(a2, back, 1), a3)
                    for parity, pixel, value in ((0, 0, c0), (0, 1, c1), (1, 0, c2), (1, 1, c3)):
                        t_ref[k, 4 + 2 * xh + pixel, parity, side, half, PAD : PAD + span, :] = value
            return carry

        lax.fori_loop(0, 4, column, 0)

        def surround(at, carry):
            x_low, parity = at // 2, at % 2
            rows_at = slice(PAD, PAD + span)
            order = [(0, 0), (0, 1), (1, 0), (1, 1)]
            left = [pltpu.roll(t_ref[k, 8 + x_low, parity, s, h, rows_at, :], channels, 1) for s, h in order]
            right = [pltpu.roll(t_ref[k, 4 + x_low, parity, s, h, rows_at, :], LANES - channels, 1) for s, h in order]
            for n, (s, h) in enumerate(order):
                before = left[n - 1] if n else jnp.zeros_like(left[0])
                after = right[n + 1] if n < 3 else jnp.zeros_like(right[0])
                t_ref[k, x_low, parity, s, h, rows_at, :] = jnp.where(slot == 0, before, left[n])
                t_ref[k, 12 + x_low, parity, s, h, rows_at, :] = jnp.where(slot == per - 1, after, right[n])
            return carry

        @pl.when(k < sections)
        def _():
            lax.fori_loop(0, 8, surround, 0)

        return carry

    lax.fori_loop(0, sections + 1, encode, 0)

    scale = SHARPNESS / channels * math.log2(math.e)
    sub8 = lax.broadcasted_iota(jnp.int32, (8, LANES), 0)
    lane8 = lane_index((8, LANES))
    wide = lane_index((1, WIDE))
    x_of = (wide // 8) % 4
    y_of = 2 * (wide % 4) + (wide // 4) % 2
    row_at = 2 * lax.broadcasted_iota(jnp.int32, (2, 8, WIDE), 1) + lax.broadcasted_iota(jnp.int32, (2, 8, WIDE), 0)
    row_weight = row_at.astype(jnp.float32)
    row_mask = jnp.where((row_at >= y_of) & (row_at <= y_of + 2 * REACH), 1.0, 0.0)
    pick = channels * ((lane8 // 8) % 4) + 8 * (lane8 % 4) + 4 * (sub8 % 2) + sub8 // 2
    patch = [jnp.where(slot == q, 1.0, 0.0).astype(jnp.bfloat16) for q in range(per)]

    def gather(values, index):
        return jnp.take_along_axis(values, index, axis=1, mode="promise_in_bounds")

    starts = [0]
    for k in range(1, sections + 1):
        starts.append(starts[-1] + pl.cdiv(rows + 2 * REACH * (sections - k), 16))
    blocks = starts[-1]

    def place(t):
        t = jnp.clip(t, 0, blocks - 1)
        k, first = 1, 0
        for n in range(1, sections):
            k = k + jnp.where(t >= starts[n], 1, 0)
            first = jnp.where(t >= starts[n], starts[n], first)
        return k, 2 * (t - first)

    def scores(k, i, side, h):
        lhs, rhs = [], []
        for half in range(2):
            window = t_ref[k - 1, 4 * h : 4 * h + 12, :, side, half, pl.ds(PAD + 1 + 4 * i, 8), :]
            lhs.append(window.reshape(12 * 16, LANES).astype(jnp.bfloat16))
            even = t_ref[k, 4 + 4 * h : 8 + 4 * h, 0, side, half, pl.ds(PAD + 1 + 4 * i, 8), :]
            odd = t_ref[k, 4 + 4 * h : 8 + 4 * h, 1, side, half, pl.ds(PAD - 3 + 4 * i, 8), :]
            current = jnp.where(sub8 < 4, even, odd) * scale
            current = current.reshape(32, LANES).astype(jnp.bfloat16)
            nothing = jnp.zeros_like(current)
            for q in range(per):
                masked = current * patch[q]
                rhs.append(jnp.concatenate([masked, nothing] if half == 0 else [nothing, masked], axis=1))
        lhs = jnp.concatenate(lhs, axis=1)
        rhs = jnp.concatenate(rhs, axis=0)
        return lax.dot_general(lhs, rhs, (((1,), (1,)), ((), ())), preferred_element_type=jnp.float32)

    def means(at):
        running = jnp.zeros((2, 8, WIDE), jnp.float32)
        moment = jnp.zeros((2, 8, WIDE), jnp.float32)
        for u in range(11, -1, -1):
            term = jnp.exp2(s_ref[at, 16 * u : 16 * u + 16, :]).reshape(2, 8, WIDE)
            if u < 3:
                term = jnp.where(x_of <= u, term, 0.0)
            if u > 8:
                term = jnp.where(x_of >= u - 8, term, 0.0)
            running = running + term
            if u:
                moment = moment + running
        running = running * row_mask
        moment = moment * row_mask
        total = jnp.sum(running[0] + running[1], axis=0, keepdims=True)
        moved = running * row_weight
        y_sum = jnp.sum(moved[0] + moved[1], axis=0, keepdims=True)
        x_sum = jnp.sum(moment[0] + moment[1], axis=0, keepdims=True)
        return y_sum / total, x_sum / total

    def compose(k, i, down, across):
        extra = REACH * (sections - k)
        whole = jnp.floor(across)
        part = across - whole
        left = lane8 + whole.astype(jnp.int32)
        right = left + 1
        left_weight = jnp.where((left >= 0) & (left < LANES), 1.0 - part, 0.0)
        right_weight = jnp.where((right >= 0) & (right < LANES), part, 0.0)
        left = jnp.clip(left, 0, LANES - 1)
        right = jnp.clip(right, 0, LANES - 1)
        sums = [down, across]
        shift = jnp.where(k == 1, FIELD_HALO - REACH * sections, 0)
        for step in range(-REACH, REACH + 1):
            row_part = jnp.maximum(0.0, 1.0 - jnp.abs(down - step))
            for c in range(2):
                values = f_ref[k - 1, c, pl.ds(8 * i + REACH + step + shift, 8), :]
                mixed = left_weight * gather(values, left) + right_weight * gather(values, right)
                sums[c] = sums[c] + row_part * mixed
        row = sub8 + 8 * i - extra + tile * rows
        inside = (row >= 0) & (row < total_rows)
        return [jnp.where(inside, value, 0.0) for value in sums]

    def step(t, carry):
        k, i = place(t)
        k_last, i_last = place(t - 2)
        found = []
        for n in range(2):
            down = jnp.zeros((8, LANES), jnp.float32)
            across = jnp.zeros((8, LANES), jnp.float32)
            for side in range(2):
                for h in range(2):
                    at = 4 * n + 2 * side + h
                    y_mean, x_mean = means(at)
                    s_ref[at] = scores(k, i + n, side, h)
                    for half in range(2):
                        keep = (lane8 // 64 == side) & ((lane8 // 32) % 2 == half) & ((lane8 // 4) % 2 == h)
                        cols = slice(LANES * half, LANES * (half + 1))
                        down = jnp.where(keep, gather(jnp.broadcast_to(y_mean[:, cols], (8, LANES)), pick), down)
                        across = jnp.where(keep, gather(jnp.broadcast_to(x_mean[:, cols], (8, LANES)), pick), across)
            found.append(down - (REACH + sub8).astype(jnp.float32))
            found.append(across - (REACH + lane8 % 4).astype(jnp.float32))
        fields = [compose(k_last, i_last + n, carry[2 * n], carry[2 * n + 1]) for n in range(2)]
        for n in range(2):
            for c in range(2):
                f_ref[k_last, c, pl.ds(pl.multiple_of(8 * i_last + 8 * n, 8), 8), :] = fields[n][c]
        return tuple(found)

    s_ref[...] = jnp.zeros_like(s_ref)
    lax.fori_loop(0, blocks + 2, step, (jnp.zeros((8, LANES), jnp.float32),) * 4)
    for k in range(1, sections + 1):
        extra = REACH * (sections - k)
        out_ref[k - 1] = f_ref[k, :, extra : extra + rows, :]


def on_device(images, section_order, prev_field, conv1_weight, conv1_bias, conv2_weight, conv2_bias):
    count = lax.axis_size("tile")
    forward = [(i, i + 1) for i in range(count - 1)]
    backward = [(target, source) for source, target in forward]
    pixel_rows, columns = images.shape[1:]
    sections = section_order.shape[0]
    rows = prev_field.shape[1]
    channels = conv1_weight.shape[0]

    def packed(picture, field):
        high = lax.reduce_precision(field, 8, 7)
        field = jnp.concatenate([high, field - high], axis=2).astype(jnp.bfloat16)
        return jnp.concatenate([picture.reshape(-1, columns), field.reshape(-1, columns)], axis=0)

    lo = lax.ppermute(packed(images[:, pixel_rows - HALO :], prev_field[:, rows - FIELD_HALO :]), "tile", forward)
    hi = lax.ppermute(packed(images[:, :HALO], prev_field[:, :FIELD_HALO]), "tile", backward)

    vmem = pl.BlockSpec(memory_space=pltpu.VMEM)
    w1, w2, b2 = pl.pallas_call(
        prepare,
        out_shape=(
            jax.ShapeDtypeStruct((WINDOWS, WIDE, WIDE), jnp.bfloat16),
            jax.ShapeDtypeStruct((WIDE, WIDE), jnp.bfloat16),
            jax.ShapeDtypeStruct((8, LANES), jnp.float32),
        ),
        in_specs=[vmem] * 5,
        out_specs=(vmem,) * 3,
        cost_estimate=pl.CostEstimate(flops=10**9, bytes_accessed=10**6, transcendentals=0),
        name="weights",
    )(jnp.asarray(first_layer_lanes()), conv1_weight, conv1_bias[None], conv2_weight, conv2_bias[None])

    groups = columns // (4 * WINDOWS)
    span = (rows + 2 * REACH * sections) // 2 + 4
    return pl.pallas_call(
        functools.partial(kernel, sections, rows, rows * count, channels),
        out_shape=jax.ShapeDtypeStruct((sections, 2, rows, prev_field.shape[2]), jnp.float32),
        in_specs=[pl.BlockSpec(memory_space=pltpu.SMEM)] + [vmem] * 7,
        out_specs=vmem,
        scratch_shapes=[
            pltpu.VMEM((2, 2 * rows + 96, LANES), jnp.float32),
            pltpu.VMEM((groups * span, WIDE), jnp.bfloat16),
            pltpu.VMEM((groups, span + 2 * PAD, LANES), jnp.float32),
            pltpu.VMEM((2, groups, span, LANES), jnp.float32),
            pltpu.VMEM((sections + 1, 16, 2, 2, 2, span + 2 * PAD, LANES), jnp.float32),
            pltpu.VMEM((sections + 1, 2, rows + 2 * FIELD_HALO + 8, LANES), jnp.float32),
            pltpu.VMEM((8, 192, WIDE), jnp.float32),
        ],
        compiler_params=pltpu.CompilerParams(vmem_limit_bytes=60 * 1024 * 1024),
        name="align",
    )(section_order, images, lo, hi, prev_field, w1, w2, b2)


def solution(mesh):
    in_specs = (P("parts", "tile", None), P("parts"), P("parts", "tile", None), P(), P(), P(), P())
    out_specs = P("parts", None, "tile", None)
    return jax.shard_map(on_device, mesh=mesh, in_specs=in_specs, out_specs=out_specs, check_vma=False)
```

time: 76.9 us -> 53.1 us (0.69); the launches traced: 75.7 us -> 52.8 us
  Pallas kernels: 53.5 us -> 42.8 us
  starting transfers between devices: 12.1 us -> 5.63 us
  local copies, waits for them, and re-layouts: 6.61 us -> 2.21 us
  matrix products: 1.9 us -> 0 us
  waiting for transfers between devices: 0.01 us -> 1.34 us
    pallas_call x1, Pallas kernels: 53.5 us -> 40.1 us  [on_device(): pl.pallas_call(functools.partial(kernel, sections, rows, rows * count, ch...]
    ppermute x4 -> x2, starting transfers between devices: 12.1 us -> 5.63 us  [the longest x1 3.71 us: on_device(): lax.ppermute(packed(images[:, pixel_rows - HALO:], prev_field[:, rows - F...]
    pallas_call x0 -> x1, Pallas kernels: none -> 2.68 us  [on_device(): pl.pallas_call(prepare, out_shape=(jax.ShapeDtypeStruct((WINDOWS, WIDE, W...]
    dot_general x2 -> x0, matrix products: 1.9 us -> none  [the longest x1 1.18 us: on_device(): jnp.einsum('bdt,toc->bcdo', jnp.asarray(second_layer_selector(), jnp.bflo...]
    convert_element_type x2 -> x0, local copies, waits for them, and re-layouts: 1.78 us -> none  [the longest x1 1.31 us: on_device(): w1 = w1.astype(jnp.bfloat16).reshape(WINDOWS, WIDE, WIDE)]
    ppermute x4 -> x2, waiting for transfers between devices: 0.01 us -> 1.34 us  [the longest x1 1.34 us: on_device(): lax.ppermute(packed(images[:, :HALO], prev_field[:, :FIELD_HALO]), 'tile'...]
    another operation x4 -> x0, local copies, waits for them, and re-layouts: 1.31 us -> none  [the longest x2 0.74 us: on_device(): rest = jnp.tile(conv1_bias, slots)]
    reshape x1 -> x0, local copies, waits for them, and re-layouts: 1.03 us -> none  [on_device(): w2 = jnp.einsum('bdt,toc->bcdo', jnp.asarray(second_layer_selector(), jnp...]
  transfers between devices with their start and end apart: 4 -> 2, of which waited for: 0 -> 1; matrix products, arithmetic and copies ran while one was open for 11% -> 1% of each run, Pallas kernels for 0% -> 5%
where the time goes in v1:
time: 53.1 us; the launch traced here: 52.8 us
  Pallas kernels  42.8 us (81%)
  starting transfers between devices  5.63 us (11%)
  local copies, waits for them, and re-layouts  2.21 us (4%)
  waiting for transfers between devices  1.34 us (3%)
  other arithmetic  0.76 us (1%)
    pallas_call x1, Pallas kernels, on_device(): pl.pallas_call(functools.partial(kernel, sections, rows, rows * count, ch...  40.1 us
    ppermute x1, starting transfers between devices, on_device(): lax.ppermute(packed(images[:, pixel_rows - HALO:], prev_field[:, rows - F...  3.71 us
    pallas_call x1, Pallas kernels, on_device(): pl.pallas_call(prepare, out_shape=(jax.ShapeDtypeStruct((WINDOWS, WIDE, W...  2.68 us
    ppermute x1, starting transfers between devices, on_device(): lax.ppermute(packed(images[:, :HALO], prev_field[:, :FIELD_HALO]), 'tile'...  1.92 us
    ppermute x1, waiting for transfers between devices, on_device(): lax.ppermute(packed(images[:, :HALO], prev_field[:, :FIELD_HALO]), 'tile'...  1.34 us
    unnamed x7, local copies, waits for them, and re-layouts  1.33 us
  transfers between devices with their start and end apart: 2, of which 1 were waited for; matrix products, arithmetic and copies ran while one was open for 1% of the time, Pallas kernels for 5%

profile of v1, /device:TPU:21, one launch (start us, length us, event | category | flops | bytes accessed | tf_op | source)
XLA Modules:
  0.0 52.8 jit_solution(7016057232918284004)
XLA Ops:
  0.0 0.7 %reduce-precision_convert_fusion = (bf16[2,16,128]{2,1,0:T(8,128)(2,1)S(1)}, bf16[2,16,128]{2,1,0:T(8,128)(2,1)S(1)}, bf16[2,16,128]{2,1,0:T(8,128)(2,1)S(1)}, bf16[2,16,128]{2,1,0:T(8,128)(2,1)S(1)}) fusion(f32[2,128,128]{2,1,0:T(8,128)} %fld_ref.1), kind=kLoop, calls=%fused_computation.3 | loop fusion | flops 32768 | bytes 65536 | tf_op jit(solution)/shard_map/convert.3
  0.7 0.9 %fusion.2 = (bf16[4,32,256]{2,1,0:T(8,128)(2,1)S(1)}, bf16[4,32,256]{2,1,0:T(8,128)(2,1)S(1)}) fusion(bf16[4,256,256]{2,1,0:T(8,128)(2,1)} %img_ref.1), kind=kLoop, calls=%fused_computation.8 | loop fusion | bytes 262144 | tf_op jit(solution)/shard_map/slice | solution.py:343
  1.6 3.7 %collective-permute-start = (bf16[160,256]{1,0:T(8,128)(2,1)S(1)}, bf16[160,256]{1,0:T(8,128)(2,1)S(1)}, u32[]{:S(2)}, u32[]{:S(2)}) collective-permute-start(bf16[160,256]{1,0:T(8,128)(2,1)S(1)} %maximum_maximum_fusion), channel_id=1, source_target_pairs={{0,1},{1,2},{2,3},{3,4},{4,5},{5,6},{6,7},{7,8},{8,9},{9,10},{10,1... | collective-permute-start | bytes 245768 | tf_op jit(solution)/shard_map/ppermute | solution.py:342
  5.4 0.0 copy-start.2
  5.4 1.9 %collective-permute-start.1 = (bf16[160,256]{1,0:T(8,128)(2,1)S(1)}, bf16[160,256]{1,0:T(8,128)(2,1)S(1)}, u32[]{:S(2)}, u32[]{:S(2)}) collective-permute-start(bf16[160,256]{1,0:T(8,128)(2,1)S(1)} %maximum_maximum_fusion.1), channel_id=1, source_target_pairs={{1,0},{2,1},{3,2},{4,3},{5,4},{6,5},{7,6},{8,7},{9,8},{10,9},{11,1... | collective-permute-start | bytes 245768 | tf_op jit(solution)/shard_map/ppermute | solution.py:343
  7.3 0.0 copy-done.2
  7.3 0.7 %copy.9.c1_ref = bf16[32,9]{1,0:T(8,128)(2,1)} copy(bf16[32,9]{0,1:T(8,128)(2,1)S(1)} %copy-done.2) | data formatting | bytes 1152 | tf_op args[3]
  8.0 2.7 %weights.1 = (bf16[8,256,256]{2,1,0:T(8,128)(2,1)}, bf16[256,256]{1,0:T(8,128)(2,1)}, f32[8,128]{1,0:T(8,128)}) custom-call(s32[1,128]{1,0:T(1,128)} %constant.2.clone.lanes_ref, bf16[32,9]{1,0:T(8,128)(2,1)} %copy.9.c1_ref, f32[1,32]{1,0:T(1,128)} %bitcast.14, bf16[9,32,32]{2,1,0:T(8,128)(2,1)} %c2_ref.1, f32[1,32]{1,0:T(1,128)} %bitcast.15), custom_call_target="tpu_custom_call" | custom-call | flops 1000000000 | bytes 1000000 | tf_op jit(solution)/shard_map/weights/pallas_call | solution.py:346
  10.7 0.0 collective-permute-done.lo_ref
  10.7 0.0 copy-start
  10.7 1.3 %collective-permute-done.1.hi_ref = bf16[160,256]{1,0:T(8,128)(2,1)S(1)} collective-permute-done((bf16[160,256]{1,0:T(8,128)(2,1)S(1)}, bf16[160,256]{1,0:T(8,128)(2,1)S(1)}, u32[]{:S(2)}, u32[]{:S(2)}) %collective-permute-start.1) | collective-permute-done | bytes 81952 | tf_op jit(solution)/shard_map/ppermute | solution.py:343
  12.1 0.0 copy-start.1
  12.1 0.0 copy-done
  12.1 0.6 %copy-done.1 = bf16[160,256]{1,0:T(8,128)(2,1)} copy-done((bf16[160,256]{1,0:T(8,128)(2,1)}, bf16[160,256]{1,0:T(8,128)(2,1)S(1)}, u32[]{:S(2)}) %copy-start.1) | copy-done | bytes 81944
  12.7 40.1 %align.1 = f32[3,2,128,128]{3,2,1,0:T(8,128)} custom-call(s32[3]{0:T(128)} %order_ref.1, bf16[4,256,256]{2,1,0:T(8,128)(2,1)} %img_ref.1, bf16[160,256]{1,0:T(8,128)(2,1)} %copy-done, bf16[160,256]{1,0:T(8,128)(2,1)} %copy-done.1, f32[2,128,128]{2,1,0:T(8,128)} %fld_ref.1, bf16[8,256,256]{2,1,0:T(8,128)(2,1)} %get-tuple-element.8.w1_ref, ...), custom_call_target="tpu_custom_call" | custom-call | tf_op jit(solution)/shard_map/align/pallas_call | solution.py:361
  (2 shorter events, 0.0 us)
Async XLA Ops:
  1.6 9.1 %collective-permute-start = (bf16[160,256]{1,0:T(8,128)(2,1)S(1)}, bf16[160,256]{1,0:T(8,128)(2,1)S(1)}, u32[]{:S(2)}, u32[]{:S(2)}) collective-permute-start(bf16[160,256]{1,0:T(8,128)(2,1)S(1)} %maximum_maximum_fusion), channel_id=1, source_target_pairs={{0,1},{1,2},{2,3},{3,4},{4,5},{5,6},{6,7},{7,8},{8,9},{9,10},{10,1... | collective-permute-start | bytes 245768 | tf_op jit(solution)/shard_map/ppermute | solution.py:342
  5.4 2.0 %copy-start.2 = (bf16[32,9]{0,1:T(8,128)(2,1)S(1)}, bf16[32,9]{0,1:T(8,128)(2,1)}, u32[]{:S(2)}) copy-start(bf16[32,9]{0,1:T(8,128)(2,1)} %param.11) | copy-start | bytes 1732
  5.4 6.7 %collective-permute-start.1 = (bf16[160,256]{1,0:T(8,128)(2,1)S(1)}, bf16[160,256]{1,0:T(8,128)(2,1)S(1)}, u32[]{:S(2)}, u32[]{:S(2)}) collective-permute-start(bf16[160,256]{1,0:T(8,128)(2,1)S(1)} %maximum_maximum_fusion.1), channel_id=1, source_target_pairs={{1,0},{2,1},{3,2},{4,3},{5,4},{6,5},{7,6},{8,7},{9,8},{10,9},{11,1... | collective-permute-start | bytes 245768 | tf_op jit(solution)/shard_map/ppermute | solution.py:343
  10.7 1.3 %copy-start = (bf16[160,256]{1,0:T(8,128)(2,1)}, bf16[160,256]{1,0:T(8,128)(2,1)S(1)}, u32[]{:S(2)}) copy-start(bf16[160,256]{1,0:T(8,128)(2,1)S(1)} %collective-permute-done.lo_ref) | copy-start | bytes 245764
  12.1 0.6 %copy-start.1 = (bf16[160,256]{1,0:T(8,128)(2,1)}, bf16[160,256]{1,0:T(8,128)(2,1)S(1)}, u32[]{:S(2)}) copy-start(bf16[160,256]{1,0:T(8,128)(2,1)S(1)} %collective-permute-done.1.hi_ref) | copy-start | bytes 245764

commit v2 on v1

--- a/solution.py
+++ b/solution.py
@@ -86,7 +86,12 @@
     for tap in range(taps):
         block = repeated(c2_ref[tap], ((0,), (0,)))
         table = jnp.where(tap_at == tap, jnp.concatenate([block] * (WIDE // channels), axis=0), table)
-    w2_ref[...] = table.astype(jnp.bfloat16)
+    table = table.astype(jnp.bfloat16)
+    for skew in range(LANES // channels):
+        for half in range(2):
+            cols = slice(LANES * half, LANES * (half + 1))
+            part = table[:, cols]
+            w2_ref[skew, :, cols] = pltpu.roll(part, channels * skew, 1) if skew else part
 
 
 def lane_index(shape):
@@ -96,9 +101,9 @@
 def kernel(
     sections, rows, total_rows, channels,
     order_ref, img_ref, lo_ref, hi_ref, fld_ref, w1_ref, w2_ref, b2_ref,
-    out_ref, z_ref, x_ref, a_ref, o_ref, t_ref, f_ref, s_ref,
+    out_ref, z_ref, x_ref, p0_ref, p1_ref, t_ref, f_ref, s_ref,
 ):
-    groups = a_ref.shape[0]
+    groups = p0_ref.shape[1]
     span = x_ref.shape[0] // groups
     per = LANES // channels
     lane = lane_index((1, LANES))
@@ -113,6 +118,67 @@
         for c in range(2):
             both = ref[pictures + FIELD_HALO * c : pictures + FIELD_HALO * (c + 1), :].astype(jnp.float32)
             f_ref[0, c, start : start + FIELD_HALO, :] = both[:, :LANES] + both[:, LANES:]
+
+    def inside_mask(k):
+        pair = lax.broadcasted_iota(jnp.int32, (span, LANES), 0) + tile * (rows // 2) - 1
+        pair = pair - REACH * (sections - k) // 2
+        return jnp.where((pair >= 0) & (pair < pairs_total), 1.0, 0.0)
+
+    def layers(xh, target):
+        for part in range(2):
+            first = jnp.dot(x_ref[...], w1_ref[xh + 4 * part], preferred_element_type=jnp.float32)
+            first = jnp.maximum(first, 0.0)
+            edge = (lane_index((1, WIDE)) // channels) % 4
+            if xh == 0 and part == 0:
+                first = jnp.concatenate([jnp.where(edge == 0, 0.0, first[:span]), first[span:]], axis=0)
+            if xh == 3 and part == 1:
+                first = jnp.concatenate([first[:-span], jnp.where(edge == 3, 0.0, first[-span:])], axis=0)
+            first = first.astype(jnp.bfloat16)
+            for odd in range(2):
+                half = groups * span // 2
+                second = jnp.dot(
+                    first[half * odd : half * (odd + 1)], w2_ref[part + 2 * odd], preferred_element_type=jnp.float32
+                )
+                at = groups // 2 * odd
+                target[part, at : at + groups // 2, PAD : PAD + span, :] = second.reshape(groups // 2, span, WIDE)
+
+    def features(k, xh, source):
+        valid = inside_mask(k)
+        for side in range(2):
+            for half in range(2):
+                parts = []
+                for q in range(per):
+                    part, odd = q % 2, q // 2
+                    at = (source, part, 2 * side + half + 4 * odd)
+                    above = at[0][at[1], at[2], PAD - 1 : PAD - 1 + span, 0:LANES]
+                    below = at[0][at[1], at[2], PAD + 1 : PAD + 1 + span, 0:LANES]
+                    here = at[0][at[1], at[2], PAD : PAD + span, LANES:WIDE]
+                    summed = here + jnp.where((slot + per - q) % per < 2, above, below)
+                    parts.append(jnp.tanh(summed + b2_ref[0:1, :]) * valid)
+                for t in range(per):
+                    value = parts[0]
+                    for q in range(1, per):
+                        value = jnp.where(slot == (t + q) % per, parts[q], value)
+
+                    def turned(by):
+                        by = channels * (by - t) % LANES
+                        return pltpu.roll(value, by, 1) if by else value
+
+                    parity, pixel = t // 2, t % 2
+                    column = 2 * xh + pixel
+                    lines = slice(PAD, PAD + span)
+                    t_ref[k, 4 + column, parity, side, half, lines, :] = turned(0)
+                    n = 2 * side + half
+                    step, edge, border = (1, 0, column - 4) if xh >= 2 else (-1, per - 1, 12 + column)
+                    moved = turned(step)
+                    own = t_ref.at[k, border, parity, side, half, lines, :]
+                    if 0 <= n + step < 4:
+                        other = t_ref.at[k, border, parity, (n + step) // 2, (n + step) % 2, lines, :]
+                        pltpu.store(other, moved, mask=jnp.broadcast_to(slot == edge, moved.shape))
+                    if 0 <= n - step < 4:
+                        pltpu.store(own, moved, mask=jnp.broadcast_to(slot != edge, moved.shape))
+                    else:
+                        own[...] = jnp.where(slot == edge, 0.0, moved)
 
     def encode(k, carry):
         extra = REACH * (sections - k)
@@ -124,11 +190,10 @@
             z_ref[half, pl.ds(base, HALO), :] = lo_ref[border, cols].astype(jnp.float32)
             z_ref[half, pl.ds(base + HALO, 2 * rows), :] = img_ref[section, :, cols].astype(jnp.float32)
             z_ref[half, pl.ds(base + HALO + 2 * rows, HALO), :] = hi_ref[border, cols].astype(jnp.float32)
-        pair = lax.broadcasted_iota(jnp.int32, (span, LANES), 0) + tile * (rows // 2) - 1 - extra // 2
-        valid = jnp.where((pair >= 0) & (pair < pairs_total), 1.0, 0.0)
-
+        valid = inside_mask(k)
         for group in range(groups):
             side, place = divmod(group, groups // 2)
+            at = group // 2 + groups // 2 * (group % 2)
             pieces = []
             for row in range(5):
                 here = z_ref[side, pl.ds(HALO - 5 + row, span, stride=4), :]
@@ -141,70 +206,20 @@
                         here = jnp.where(lane < LANES // 2, low, high)
                 start = PITCH * (row % 3)
                 shift = (start - (2 * LANES // groups * place - 3)) % LANES
-                pieces.append(pltpu.roll(here, shift, 1))
+                pieces.append(pltpu.roll(here.astype(jnp.bfloat16), shift, 1))
             left = jnp.where(lane < PITCH, pieces[0], jnp.where(lane < 2 * PITCH, pieces[1], pieces[2]))
-            right = jnp.where(lane < PITCH, pieces[3], jnp.where(lane < BIAS_LANE - LANES, pieces[4], valid))
-            x_ref[pl.ds(span * group, span), 0:LANES] = (left * valid).astype(jnp.bfloat16)
-            x_ref[pl.ds(span * group, span), LANES:WIDE] = (right * valid).astype(jnp.bfloat16)
-
-        def column(xh, carry):
-            for part in range(2):
-                window = xh + 4 * part
-                first = jnp.dot(x_ref[...], w1_ref[window], preferred_element_type=jnp.float32)
-                first = jnp.maximum(first, 0.0).reshape(groups, span, WIDE)
-                edge = (lane_index((1, 1, WIDE)) // channels) % 4
-                group_at = lax.broadcasted_iota(jnp.int32, (groups, 1, WIDE), 0)
-                if part == 0:
-                    drop = (edge == 0) & (group_at == 0) & (xh == 0)
-                else:
-                    drop = (edge == 3) & (group_at == groups - 1) & (xh == 3)
-                first = jnp.where(drop, 0.0, first)
-                first = first.reshape(groups * span, WIDE).astype(jnp.bfloat16)
-                second = jnp.dot(first, w2_ref[...], preferred_element_type=jnp.float32)
-                second = second.reshape(groups, span, WIDE)
-                a_ref[:, PAD : PAD + span, :] = second[:, :, 0:LANES]
-                for group in range(groups):
-                    above = a_ref[group, PAD - 1 : PAD - 1 + span, :]
-                    below = a_ref[group, PAD + 1 : PAD + 1 + span, :]
-                    summed = second[group, :, LANES:WIDE] + jnp.where(lane < LANES // 2, above, below)
-                    o_ref[part, group] = jnp.tanh(summed + b2_ref[0:1, :]) * valid
-            for side in range(2):
-                for half in range(2):
-                    at = 4 * side + 2 * half
-                    s0, s1, s2, s3 = o_ref[0, at], o_ref[1, at], o_ref[0, at + 1], o_ref[1, at + 1]
-                    low = lane < LANES // 2
-                    even = slot % 2 == 0
-                    a0, a2 = jnp.where(low, s0, pltpu.roll(s2, 64, 1)), jnp.where(low, pltpu.roll(s0, 64, 1), s2)
-                    a1, a3 = jnp.where(low, s1, pltpu.roll(s3, 64, 1)), jnp.where(low, pltpu.roll(s1, 64, 1), s3)
-                    back = LANES - channels
-                    c0, c1 = jnp.where(even, a0, pltpu.roll(a1, channels, 1)), jnp.where(even, pltpu.roll(a0, back, 1), a1)
-                    c2, c3 = jnp.where(even, a2, pltpu.roll(a3, channels, 1)), jnp.where(even, pltpu.roll(a2, back, 1), a3)
-                    for parity, pixel, value in ((0, 0, c0), (0, 1, c1), (1, 0, c2), (1, 1, c3)):
-                        t_ref[k, 4 + 2 * xh + pixel, parity, side, half, PAD : PAD + span, :] = value
-            return carry
-
-        lax.fori_loop(0, 4, column, 0)
-
-        def surround(at, carry):
-            x_low, parity = at // 2, at % 2
-            rows_at = slice(PAD, PAD + span)
-            order = [(0, 0), (0, 1), (1, 0), (1, 1)]
-            left = [pltpu.roll(t_ref[k, 8 + x_low, parity, s, h, rows_at, :], channels, 1) for s, h in order]
-            right = [pltpu.roll(t_ref[k, 4 + x_low, parity, s, h, rows_at, :], LANES - channels, 1) for s, h in order]
-            for n, (s, h) in enumerate(order):
-                before = left[n - 1] if n else jnp.zeros_like(left[0])
-                after = right[n + 1] if n < 3 else jnp.zeros_like(right[0])
-                t_ref[k, x_low, parity, s, h, rows_at, :] = jnp.where(slot == 0, before, left[n])
-                t_ref[k, 12 + x_low, parity, s, h, rows_at, :] = jnp.where(slot == per - 1, after, right[n])
-            return carry
-
-        @pl.when(k < sections)
-        def _():
-            lax.fori_loop(0, 8, surround, 0)
-
+            right = jnp.where(lane < PITCH, pieces[3], jnp.where(lane < BIAS_LANE - LANES, pieces[4], valid.astype(jnp.bfloat16)))
+            x_ref[pl.ds(span * at, span), 0:LANES] = left * valid.astype(jnp.bfloat16)
+            x_ref[pl.ds(span * at, span), LANES:WIDE] = right * valid.astype(jnp.bfloat16)
+
+        buffers = (p0_ref, p1_ref)
+        for xh in range(4):
+            layers(xh, buffers[xh % 2])
+            features(k if xh else jnp.maximum(k - 1, 0), (xh - 1) % 4, buffers[(xh - 1) % 2])
         return carry
 
     lax.fori_loop(0, sections + 1, encode, 0)
+    features(sections, 3, p1_ref)
 
     scale = SHARPNESS / channels * math.log2(math.e)
     sub8 = lax.broadcasted_iota(jnp.int32, (8, LANES), 0)
@@ -347,7 +362,7 @@
         prepare,
         out_shape=(
             jax.ShapeDtypeStruct((WINDOWS, WIDE, WIDE), jnp.bfloat16),
-            jax.ShapeDtypeStruct((WIDE, WIDE), jnp.bfloat16),
+            jax.ShapeDtypeStruct((LANES // channels, WIDE, WIDE), jnp.bfloat16),
             jax.ShapeDtypeStruct((8, LANES), jnp.float32),
         ),
         in_specs=[vmem] * 5,
@@ -366,8 +381,8 @@
         scratch_shapes=[
             pltpu.VMEM((2, 2 * rows + 96, LANES), jnp.float32),
             pltpu.VMEM((groups * span, WIDE), jnp.bfloat16),
-            pltpu.VMEM((groups, span + 2 * PAD, LANES), jnp.float32),
-            pltpu.VMEM((2, groups, span, LANES), jnp.float32),
+            pltpu.VMEM((2, groups, span + 2 * PAD, WIDE), jnp.float32),
+            pltpu.VMEM((2, groups, span + 2 * PAD, WIDE), jnp.float32),
             pltpu.VMEM((sections + 1, 16, 2, 2, 2, span + 2 * PAD, LANES), jnp.float32),
             pltpu.VMEM((sections + 1, 2, rows + 2 * FIELD_HALO + 8, LANES), jnp.float32),
             pltpu.VMEM((8, 192, WIDE), jnp.float32),

time: 53.1 us -> 42.3 us (0.80)
  Pallas kernels: 42.8 us -> 32.1 us
    pallas_call x1, Pallas kernels: 40.1 us -> 29.3 us  [on_device(): pl.pallas_call(functools.partial(kernel, sections, rows, rows * count, ch...]
  transfers between devices with their start and end apart: 2 -> 2, of which waited for: 1 -> 1; matrix products, arithmetic and copies ran while one was open for 1% -> 2% of each run, Pallas kernels for 5% -> 7%
where the time goes in v2:
time: 42.3 us; the launch traced here: 41.9 us
  Pallas kernels  32.1 us (76%)
  starting transfers between devices  5.63 us (13%)
  local copies, waits for them, and re-layouts  2.21 us (5%)
  waiting for transfers between devices  1.21 us (3%)
  other arithmetic  0.76 us (2%)
    pallas_call x1, Pallas kernels, on_device(): pl.pallas_call(functools.partial(kernel, sections, rows, rows * count, ch...  29.3 us
    ppermute x1, starting transfers between devices, on_device(): lax.ppermute(packed(images[:, pixel_rows - HALO:], prev_field[:, rows - F...  3.71 us
    pallas_call x1, Pallas kernels, on_device(): pl.pallas_call(prepare, out_shape=(jax.ShapeDtypeStruct((WINDOWS, WIDE, W...  2.82 us
    ppermute x1, starting transfers between devices, on_device(): lax.ppermute(packed(images[:, :HALO], prev_field[:, :FIELD_HALO]), 'tile'...  1.92 us
    unnamed x7, local copies, waits for them, and re-layouts  1.32 us
    ppermute x1, waiting for transfers between devices, on_device(): lax.ppermute(packed(images[:, :HALO], prev_field[:, :FIELD_HALO]), 'tile'...  1.2 us
    slice x1, local copies, waits for them, and re-layouts, on_device(): images[:, :HALO]  0.88 us
  transfers between devices with their start and end apart: 2, of which 1 were waited for; matrix products, arithmetic and copies ran while one was open for 2% of the time, Pallas kernels for 7%

profile of v2, /device:TPU:21, one launch (start us, length us, event | category | flops | bytes accessed | tf_op | source)
XLA Modules:
  0.0 41.9 jit_solution(66232024783722500)
XLA Ops:
  0.0 0.7 %reduce-precision_convert_fusion = (bf16[2,16,128]{2,1,0:T(8,128)(2,1)S(1)}, bf16[2,16,128]{2,1,0:T(8,128)(2,1)S(1)}, bf16[2,16,128]{2,1,0:T(8,128)(2,1)S(1)}, bf16[2,16,128]{2,1,0:T(8,128)(2,1)S(1)}) fusion(f32[2,128,128]{2,1,0:T(8,128)} %fld_ref.1), kind=kLoop, calls=%fused_computation.3 | loop fusion | flops 32768 | bytes 65536 | tf_op jit(solution)/shard_map/convert.3
  0.7 0.9 %fusion.2 = (bf16[4,32,256]{2,1,0:T(8,128)(2,1)S(1)}, bf16[4,32,256]{2,1,0:T(8,128)(2,1)S(1)}) fusion(bf16[4,256,256]{2,1,0:T(8,128)(2,1)} %img_ref.1), kind=kLoop, calls=%fused_computation.8 | loop fusion | bytes 262144 | tf_op jit(solution)/shard_map/slice | solution.py:358
  1.6 3.7 %collective-permute-start = (bf16[160,256]{1,0:T(8,128)(2,1)S(1)}, bf16[160,256]{1,0:T(8,128)(2,1)S(1)}, u32[]{:S(2)}, u32[]{:S(2)}) collective-permute-start(bf16[160,256]{1,0:T(8,128)(2,1)S(1)} %maximum_maximum_fusion), channel_id=1, source_target_pairs={{0,1},{1,2},{2,3},{3,4},{4,5},{5,6},{6,7},{7,8},{8,9},{9,10},{10,1... | collective-permute-start | bytes 245768 | tf_op jit(solution)/shard_map/ppermute | solution.py:357
  5.4 0.0 copy-start.2
  5.4 1.9 %collective-permute-start.1 = (bf16[160,256]{1,0:T(8,128)(2,1)S(1)}, bf16[160,256]{1,0:T(8,128)(2,1)S(1)}, u32[]{:S(2)}, u32[]{:S(2)}) collective-permute-start(bf16[160,256]{1,0:T(8,128)(2,1)S(1)} %maximum_maximum_fusion.1), channel_id=1, source_target_pairs={{1,0},{2,1},{3,2},{4,3},{5,4},{6,5},{7,6},{8,7},{9,8},{10,9},{11,1... | collective-permute-start | bytes 245768 | tf_op jit(solution)/shard_map/ppermute | solution.py:358
  7.3 0.0 copy-done.2
  7.3 0.7 %copy.9.c1_ref = bf16[32,9]{1,0:T(8,128)(2,1)} copy(bf16[32,9]{0,1:T(8,128)(2,1)S(1)} %copy-done.2) | data formatting | bytes 1152 | tf_op args[3]
  8.0 2.8 %weights.1 = (bf16[8,256,256]{2,1,0:T(8,128)(2,1)}, bf16[4,256,256]{2,1,0:T(8,128)(2,1)}, f32[8,128]{1,0:T(8,128)}) custom-call(s32[1,128]{1,0:T(1,128)} %constant.2.clone.lanes_ref, bf16[32,9]{1,0:T(8,128)(2,1)} %copy.9.c1_ref, f32[1,32]{1,0:T(1,128)} %bitcast.14, bf16[9,32,32]{2,1,0:T(8,128)(2,1)} %c2_ref.1, f32[1,32]{1,0:T(1,128)} %bitcast.15), custom_call_target="tpu_custom_call" | custom-call | flops 1000000000 | bytes 1000000 | tf_op jit(solution)/shard_map/weights/pallas_call | solution.py:361
  10.8 0.0 collective-permute-done.lo_ref
  10.8 0.0 copy-start
  10.8 1.2 %collective-permute-done.1.hi_ref = bf16[160,256]{1,0:T(8,128)(2,1)S(1)} collective-permute-done((bf16[160,256]{1,0:T(8,128)(2,1)S(1)}, bf16[160,256]{1,0:T(8,128)(2,1)S(1)}, u32[]{:S(2)}, u32[]{:S(2)}) %collective-permute-start.1) | collective-permute-done | bytes 81952 | tf_op jit(solution)/shard_map/ppermute | solution.py:358
  12.1 0.0 copy-start.1
  12.1 0.0 copy-done
  12.1 0.6 %copy-done.1 = bf16[160,256]{1,0:T(8,128)(2,1)} copy-done((bf16[160,256]{1,0:T(8,128)(2,1)}, bf16[160,256]{1,0:T(8,128)(2,1)S(1)}, u32[]{:S(2)}) %copy-start.1) | copy-done | bytes 81944
  12.7 29.3 %align.1 = f32[3,2,128,128]{3,2,1,0:T(8,128)} custom-call(s32[3]{0:T(128)} %order_ref.1, bf16[4,256,256]{2,1,0:T(8,128)(2,1)} %img_ref.1, bf16[160,256]{1,0:T(8,128)(2,1)} %copy-done, bf16[160,256]{1,0:T(8,128)(2,1)} %copy-done.1, f32[2,128,128]{2,1,0:T(8,128)} %fld_ref.1, bf16[8,256,256]{2,1,0:T(8,128)(2,1)} %get-tuple-element.8.w1_ref, ...), custom_call_target="tpu_custom_call" | custom-call | tf_op jit(solution)/shard_map/align/pallas_call | solution.py:376
  (2 shorter events, 0.0 us)
Async XLA Ops:
  1.6 9.2 %collective-permute-start = (bf16[160,256]{1,0:T(8,128)(2,1)S(1)}, bf16[160,256]{1,0:T(8,128)(2,1)S(1)}, u32[]{:S(2)}, u32[]{:S(2)}) collective-permute-start(bf16[160,256]{1,0:T(8,128)(2,1)S(1)} %maximum_maximum_fusion), channel_id=1, source_target_pairs={{0,1},{1,2},{2,3},{3,4},{4,5},{5,6},{6,7},{7,8},{8,9},{9,10},{10,1... | collective-permute-start | bytes 245768 | tf_op jit(solution)/shard_map/ppermute | solution.py:357
  5.4 2.0 %copy-start.2 = (bf16[32,9]{0,1:T(8,128)(2,1)S(1)}, bf16[32,9]{0,1:T(8,128)(2,1)}, u32[]{:S(2)}) copy-start(bf16[32,9]{0,1:T(8,128)(2,1)} %param.11) | copy-start | bytes 1732
  5.4 6.7 %collective-permute-start.1 = (bf16[160,256]{1,0:T(8,128)(2,1)S(1)}, bf16[160,256]{1,0:T(8,128)(2,1)S(1)}, u32[]{:S(2)}, u32[]{:S(2)}) collective-permute-start(bf16[160,256]{1,0:T(8,128)(2,1)S(1)} %maximum_maximum_fusion.1), channel_id=1, source_target_pairs={{1,0},{2,1},{3,2},{4,3},{5,4},{6,5},{7,6},{8,7},{9,8},{10,9},{11,1... | collective-permute-start | bytes 245768 | tf_op jit(solution)/shard_map/ppermute | solution.py:358
  10.8 1.2 %copy-start = (bf16[160,256]{1,0:T(8,128)(2,1)}, bf16[160,256]{1,0:T(8,128)(2,1)S(1)}, u32[]{:S(2)}) copy-start(bf16[160,256]{1,0:T(8,128)(2,1)S(1)} %collective-permute-done.lo_ref) | copy-start | bytes 245764
  12.1 0.6 %copy-start.1 = (bf16[160,256]{1,0:T(8,128)(2,1)}, bf16[160,256]{1,0:T(8,128)(2,1)S(1)}, u32[]{:S(2)}) copy-start(bf16[160,256]{1,0:T(8,128)(2,1)S(1)} %collective-permute-done.1.hi_ref) | copy-start | bytes 245764

commit v3 on v2

--- a/solution.py
+++ b/solution.py
@@ -14,6 +14,7 @@
 LANES = 128
 WIDE = 256
 HALO = 32
+LATER = 24
 FIELD_HALO = 16
 PITCH = 40
 BIAS_LANE = 248
@@ -31,7 +32,37 @@
     return lanes
 
 
-def prepare(lanes_ref, c1_ref, b1_ref, c2_ref, b2_ref, w1_ref, w2_ref, bias_ref):
+def pack(img_ref, fld_ref, up_ref, down_ref, field_ref, sem):
+    sections = img_ref.shape[0] - 1
+    copies = []
+    for side, out_ref in enumerate((up_ref, down_ref)):
+        at = 0
+        for section in range(sections + 1):
+            count = LATER if section else HALO
+            first = 0 if side else img_ref.shape[1] - count
+            copies.append(
+                pltpu.make_async_copy(
+                    img_ref.at[section, first : first + count], out_ref.at[at : at + count], sem.at[side, section]
+                )
+            )
+            at += count
+        first = 0 if side else fld_ref.shape[1] - FIELD_HALO
+        copies.append(
+            pltpu.make_async_copy(
+                fld_ref.at[:, first : first + FIELD_HALO], field_ref.at[side], sem.at[side, sections + 1]
+            )
+        )
+    for copy in copies:
+        copy.start()
+    for copy in copies:
+        copy.wait()
+    for side, out_ref in enumerate((up_ref, down_ref)):
+        field = jnp.concatenate([field_ref[side, 0], field_ref[side, 1]], axis=1)
+        out_ref[HALO + LATER * sections :, :] = field.astype(jnp.bfloat16)
+
+
+def prepare(chain_ref, lanes_ref, c1_ref, b1_ref, c2_ref, b2_ref, w1_ref, w2_ref, bias_ref):
+    del chain_ref
     channels, taps = c1_ref.shape
 
     def indices(shape):
@@ -100,8 +131,8 @@
 
 def kernel(
     sections, rows, total_rows, channels,
-    order_ref, img_ref, lo_ref, hi_ref, fld_ref, w1_ref, w2_ref, b2_ref,
-    out_ref, z_ref, x_ref, p0_ref, p1_ref, t_ref, f_ref, s_ref,
+    chain_ref, img_ref, lo_ref, hi_ref, fld_ref, w1_ref, w2_ref, b2_ref,
+    out_ref, z_ref, x_ref, p0_ref, p1_ref, t_ref, f_ref, s0_ref, s1_ref,
 ):
     groups = p0_ref.shape[1]
     span = x_ref.shape[0] // groups
@@ -112,12 +143,12 @@
     pairs_total = total_rows // 2
 
     z_ref[...] = jnp.zeros_like(z_ref)
-    pictures = HALO * (sections + 1)
+    pictures = HALO + LATER * sections
     f_ref[0, :, FIELD_HALO : FIELD_HALO + rows, :] = fld_ref[...]
     for ref, start in ((lo_ref, 0), (hi_ref, FIELD_HALO + rows)):
         for c in range(2):
-            both = ref[pictures + FIELD_HALO * c : pictures + FIELD_HALO * (c + 1), :].astype(jnp.float32)
-            f_ref[0, c, start : start + FIELD_HALO, :] = both[:, :LANES] + both[:, LANES:]
+            part = ref[pictures : pictures + FIELD_HALO, LANES * c : LANES * (c + 1)]
+            f_ref[0, c, start : start + FIELD_HALO, :] = part.astype(jnp.float32)
 
     def inside_mask(k):
         pair = lax.broadcasted_iota(jnp.int32, (span, LANES), 0) + tile * (rows // 2) - 1
@@ -182,14 +213,25 @@
 
     def encode(k, carry):
         extra = REACH * (sections - k)
-        section = jnp.where(k == 0, 0, 1 + order_ref[jnp.maximum(k - 1, 0)])
-        border = pl.ds(pl.multiple_of(HALO * section, HALO), HALO)
-        base = pl.multiple_of(2 * extra, 8)
+        section = jnp.where(k == 0, 0, chain_ref[jnp.maximum(k - 1, 0)])
+        first = jnp.where(k == 0, 0, HALO + LATER * (section - 1))
+        low = pl.ds(pl.multiple_of(first + jnp.where(k == 0, HALO - LATER, 0), 8), LATER)
+        high = pl.ds(pl.multiple_of(first, 8), LATER)
+        base = pl.multiple_of(2 * extra + HALO, 8)
         for half in range(2):
             cols = slice(LANES * half, LANES * (half + 1))
-            z_ref[half, pl.ds(base, HALO), :] = lo_ref[border, cols].astype(jnp.float32)
-            z_ref[half, pl.ds(base + HALO, 2 * rows), :] = img_ref[section, :, cols].astype(jnp.float32)
-            z_ref[half, pl.ds(base + HALO + 2 * rows, HALO), :] = hi_ref[border, cols].astype(jnp.float32)
+            z_ref[half, pl.ds(base - LATER, LATER), :] = lo_ref[low, cols].astype(jnp.float32)
+            z_ref[half, pl.ds(base, 2 * rows), :] = img_ref[section, :, cols].astype(jnp.float32)
+            z_ref[half, pl.ds(base + 2 * rows, LATER), :] = hi_ref[high, cols].astype(jnp.float32)
+
+        @pl.when(k == 0)
+        def _():
+            for half in range(2):
+                cols = slice(LANES * half, LANES * (half + 1))
+                far = HALO - LATER
+                z_ref[half, pl.ds(base - HALO, far), :] = lo_ref[0:far, cols].astype(jnp.float32)
+                z_ref[half, pl.ds(base + 2 * rows + LATER, far), :] = hi_ref[LATER:HALO, cols].astype(jnp.float32)
+
         valid = inside_mask(k)
         for group in range(groups):
             side, place = divmod(group, groups // 2)
@@ -266,11 +308,11 @@
         rhs = jnp.concatenate(rhs, axis=0)
         return lax.dot_general(lhs, rhs, (((1,), (1,)), ((), ())), preferred_element_type=jnp.float32)
 
-    def means(at):
+    def means(source, at):
         running = jnp.zeros((2, 8, WIDE), jnp.float32)
         moment = jnp.zeros((2, 8, WIDE), jnp.float32)
         for u in range(11, -1, -1):
-            term = jnp.exp2(s_ref[at, 16 * u : 16 * u + 16, :]).reshape(2, 8, WIDE)
+            term = jnp.exp2(source[at, 16 * u : 16 * u + 16, :]).reshape(2, 8, WIDE)
             if u < 3:
                 term = jnp.where(x_of <= u, term, 0.0)
             if u > 8:
@@ -308,9 +350,18 @@
         inside = (row >= 0) & (row < total_rows)
         return [jnp.where(inside, value, 0.0) for value in sums]
 
-    def step(t, carry):
+    def fill(t, target, at):
         k, i = place(t)
-        k_last, i_last = place(t - 2)
+        target[at] = scores(k, i + at // 4, at // 2 % 2, at % 2)
+
+    def finish(t, found):
+        k, i = place(t)
+        fields = [compose(k, i + n, found[2 * n], found[2 * n + 1]) for n in range(2)]
+        for n in range(2):
+            for c in range(2):
+                f_ref[k, c, pl.ds(pl.multiple_of(8 * i + 8 * n, 8), 8), :] = fields[n][c]
+
+    def step(t, carry, source, target):
         found = []
         for n in range(2):
             down = jnp.zeros((8, LANES), jnp.float32)
@@ -318,8 +369,8 @@
             for side in range(2):
                 for h in range(2):
                     at = 4 * n + 2 * side + h
-                    y_mean, x_mean = means(at)
-                    s_ref[at] = scores(k, i + n, side, h)
+                    fill(t + 1, target, at)
+                    y_mean, x_mean = means(source, at)
                     for half in range(2):
                         keep = (lane8 // 64 == side) & ((lane8 // 32) % 2 == half) & ((lane8 // 4) % 2 == h)
                         cols = slice(LANES * half, LANES * (half + 1))
@@ -327,14 +378,18 @@
                         across = jnp.where(keep, gather(jnp.broadcast_to(x_mean[:, cols], (8, LANES)), pick), across)
             found.append(down - (REACH + sub8).astype(jnp.float32))
             found.append(across - (REACH + lane8 % 4).astype(jnp.float32))
-        fields = [compose(k_last, i_last + n, carry[2 * n], carry[2 * n + 1]) for n in range(2)]
-        for n in range(2):
-            for c in range(2):
-                f_ref[k_last, c, pl.ds(pl.multiple_of(8 * i_last + 8 * n, 8), 8), :] = fields[n][c]
+        finish(t - 1, carry)
         return tuple(found)
 
-    s_ref[...] = jnp.zeros_like(s_ref)
-    lax.fori_loop(0, blocks + 2, step, (jnp.zeros((8, LANES), jnp.float32),) * 4)
+    def two_steps(j, carry):
+        carry = step(2 * j, carry, s0_ref, s1_ref)
+        return step(2 * j + 1, carry, s1_ref, s0_ref)
+
+    for at in range(8):
+        fill(0, s0_ref, at)
+    turns = pl.cdiv(blocks, 2)
+    found = lax.fori_loop(0, turns, two_steps, (jnp.zeros((8, LANES), jnp.float32),) * 4)
+    finish(2 * turns - 1, found)
     for k in range(1, sections + 1):
         extra = REACH * (sections - k)
         out_ref[k - 1] = f_ref[k, :, extra : extra + rows, :]
@@ -349,15 +404,25 @@
     rows = prev_field.shape[1]
     channels = conv1_weight.shape[0]
 
-    def packed(picture, field):
-        high = lax.reduce_precision(field, 8, 7)
-        field = jnp.concatenate([high, field - high], axis=2).astype(jnp.bfloat16)
-        return jnp.concatenate([picture.reshape(-1, columns), field.reshape(-1, columns)], axis=0)
-
-    lo = lax.ppermute(packed(images[:, pixel_rows - HALO :], prev_field[:, rows - FIELD_HALO :]), "tile", forward)
-    hi = lax.ppermute(packed(images[:, :HALO], prev_field[:, :FIELD_HALO]), "tile", backward)
-
     vmem = pl.BlockSpec(memory_space=pltpu.VMEM)
+    hbm = pl.BlockSpec(memory_space=pl.ANY)
+    held = HALO + LATER * sections + FIELD_HALO
+    up, down = pl.pallas_call(
+        pack,
+        out_shape=(jax.ShapeDtypeStruct((held, columns), images.dtype),) * 2,
+        in_specs=[hbm, hbm],
+        out_specs=(vmem, vmem),
+        scratch_shapes=[
+            pltpu.VMEM((2, 2, FIELD_HALO, prev_field.shape[2]), jnp.float32),
+            pltpu.SemaphoreType.DMA((2, sections + 2)),
+        ],
+        compiler_params=pltpu.CompilerParams(vmem_limit_bytes=66850000),
+        name="pack",
+    )(images, prev_field)
+    chain = section_order + 1
+    lo = lax.ppermute(up, "tile", forward)
+    hi = lax.ppermute(down, "tile", backward)
+
     w1, w2, b2 = pl.pallas_call(
         prepare,
         out_shape=(
@@ -365,11 +430,12 @@
             jax.ShapeDtypeStruct((LANES // channels, WIDE, WIDE), jnp.bfloat16),
             jax.ShapeDtypeStruct((8, LANES), jnp.float32),
         ),
-        in_specs=[vmem] * 5,
+        in_specs=[pl.BlockSpec(memory_space=pltpu.SMEM)] + [vmem] * 5,
         out_specs=(vmem,) * 3,
         cost_estimate=pl.CostEstimate(flops=10**9, bytes_accessed=10**6, transcendentals=0),
+        compiler_params=pltpu.CompilerParams(vmem_limit_bytes=12 * 1024 * 1024),
         name="weights",
-    )(jnp.asarray(first_layer_lanes()), conv1_weight, conv1_bias[None], conv2_weight, conv2_bias[None])
+    )(chain, jnp.asarray(first_layer_lanes()), conv1_weight, conv1_bias[None], conv2_weight, conv2_bias[None])
 
     groups = columns // (4 * WINDOWS)
     span = (rows + 2 * REACH * sections) // 2 + 4
@@ -386,10 +452,11 @@
             pltpu.VMEM((sections + 1, 16, 2, 2, 2, span + 2 * PAD, LANES), jnp.float32),
             pltpu.VMEM((sections + 1, 2, rows + 2 * FIELD_HALO + 8, LANES), jnp.float32),
             pltpu.VMEM((8, 192, WIDE), jnp.float32),
+            pltpu.VMEM((8, 192, WIDE), jnp.float32),
         ],
-        compiler_params=pltpu.CompilerParams(vmem_limit_bytes=60 * 1024 * 1024),
+        compiler_params=pltpu.CompilerParams(vmem_limit_bytes=44 * 1024 * 1024),
         name="align",
-    )(section_order, images, lo, hi, prev_field, w1, w2, b2)
+    )(chain, images, lo, hi, prev_field, w1, w2, b2)
 
 
 def solution(mesh):

time: 42.3 us -> 38.5 us (0.910)
  Pallas kernels: 32.1 us -> 29.5 us
  local copies, waits for them, and re-layouts: 2.21 us -> 0.79 us
  waiting for transfers between devices: 1.21 us -> 2.23 us
  other arithmetic: 0.76 us -> 0.01 us
    pallas_call x1, Pallas kernels: 29.3 us -> 26.2 us  [on_device(): pl.pallas_call(functools.partial(kernel, sections, rows, rows * count, ch...]
    pallas_call x0 -> x1, Pallas kernels: none -> 1.6 us  [on_device(): pl.pallas_call(pack, out_shape=(jax.ShapeDtypeStruct((held, columns), ima...]
    pallas_call x1, Pallas kernels: 2.82 us -> 1.65 us  [on_device(): pl.pallas_call(prepare, out_shape=(jax.ShapeDtypeStruct((WINDOWS, WIDE, W...]
    ppermute x2, waiting for transfers between devices: 1.21 us -> 2.23 us  [the longest x1 2.23 us: on_device(): hi = lax.ppermute(down, 'tile', backward)]
    slice x1 -> x0, local copies, waits for them, and re-layouts: 0.88 us -> none  [on_device(): images[:, :HALO]]
    another operation x1 -> x0, other arithmetic: 0.74 us -> none
    unnamed x7 -> x17, local copies, waits for them, and re-layouts: 1.32 us -> 0.79 us
  transfers between devices with their start and end apart: 2 -> 2, of which waited for: 1 -> 1; matrix products, arithmetic and copies ran while one was open for 2% -> 0% of each run, Pallas kernels for 7% -> 4%
where the time goes in v3:
time: 38.5 us; the launch traced here: 38.2 us
  Pallas kernels  29.5 us (77%)
  starting transfers between devices  5.63 us (15%)
  waiting for transfers between devices  2.23 us (6%)
  local copies, waits for them, and re-layouts  0.79 us (2%)
    pallas_call x1, Pallas kernels, on_device(): pl.pallas_call(functools.partial(kernel, sections, rows, rows * count, ch...  26.2 us
    ppermute x1, starting transfers between devices, on_device(): lo = lax.ppermute(up, 'tile', forward)  3.71 us
    ppermute x1, waiting for transfers between devices, on_device(): hi = lax.ppermute(down, 'tile', backward)  2.23 us
    ppermute x1, starting transfers between devices, on_device(): hi = lax.ppermute(down, 'tile', backward)  1.92 us
    pallas_call x1, Pallas kernels, on_device(): pl.pallas_call(prepare, out_shape=(jax.ShapeDtypeStruct((WINDOWS, WIDE, W...  1.65 us
    pallas_call x1, Pallas kernels, on_device(): pl.pallas_call(pack, out_shape=(jax.ShapeDtypeStruct((held, columns), ima...  1.6 us
    unnamed x17, local copies, waits for them, and re-layouts  0.79 us
  transfers between devices with their start and end apart: 2, of which 1 were waited for; matrix products, arithmetic and copies ran while one was open for 0% of the time, Pallas kernels for 4%

profile of v3, /device:TPU:21, one launch (start us, length us, event | category | flops | bytes accessed | tf_op | source)
XLA Modules:
  0.0 38.2 jit_solution(11317379596726756404)
XLA Ops:
  0.0 0.0 copy-start.2
  0.0 0.0 copy-start.7
  0.0 1.6 %pack.1 = (bf16[120,256]{1,0:T(8,128)(2,1)}, bf16[120,256]{1,0:T(8,128)(2,1)}) custom-call(bf16[4,256,256]{2,1,0:T(8,128)(2,1)} %img_ref.3, f32[2,128,128]{2,1,0:T(8,128)} %fld_ref.3), custom_call_target="tpu_custom_call" | custom-call | tf_op jit(solution)/shard_map/pack/pallas_call | solution.py:410
  1.6 0.0 copy-start.6
  1.6 3.7 %collective-permute-start = (bf16[120,256]{1,0:T(8,128)(2,1)}, bf16[120,256]{1,0:T(8,128)(2,1)S(1)}, u32[]{:S(2)}, u32[]{:S(2)}) collective-permute-start(bf16[120,256]{1,0:T(8,128)(2,1)} %get-tuple-element.10), channel_id=1, source_target_pairs={{0,1},{1,2},{2,3},{3,4},{4,5},{5,6},{6,7},{7,8},{8,9},{9,10},{10,1... | collective-permute-start | bytes 184328 | tf_op jit(solution)/shard_map/ppermute | solution.py:423
  5.3 1.9 %collective-permute-start.1 = (bf16[120,256]{1,0:T(8,128)(2,1)}, bf16[120,256]{1,0:T(8,128)(2,1)S(1)}, u32[]{:S(2)}, u32[]{:S(2)}) collective-permute-start(bf16[120,256]{1,0:T(8,128)(2,1)} %get-tuple-element.11), channel_id=1, source_target_pairs={{1,0},{2,1},{3,2},{4,3},{5,4},{6,5},{7,6},{8,7},{9,8},{10,9},{11,1... | collective-permute-start | bytes 184328 | tf_op jit(solution)/shard_map/ppermute | solution.py:424
  7.3 0.0 copy-done.7
  7.3 0.0 copy-done.6
  7.3 0.1 copy.9.c1_ref
  7.4 0.0 copy-start.3
  7.4 0.0 copy-start.4
  7.4 0.0 copy-start.5
  7.4 0.0 copy-done.2
  7.4 0.6 %copy-done.3 = f32[32]{0:T(128)S(1)} copy-done((f32[32]{0:T(128)S(1)}, f32[32]{0:T(128)}, u32[]{:S(2)}) %copy-start.3) | copy-done | bytes 152
  8.1 0.0 copy-done.4
  8.1 0.0 copy-done.5
  8.1 0.0 copy-start
  8.1 0.0 copy-start.1
  8.1 1.7 %weights.1 = (bf16[8,256,256]{2,1,0:T(8,128)(2,1)S(1)}, bf16[4,256,256]{2,1,0:T(8,128)(2,1)S(1)}, f32[8,128]{1,0:T(8,128)S(1)}) custom-call(s32[3]{0:T(128)S(1)} %broadcast_add_fusion.chain_ref, s32[1,128]{1,0:T(1,128)S(1)} %copy-done.5, bf16[32,9]{1,0:T(8,128)(2,1)S(1)} %copy.9.c1_ref, f32[1,32]{1,0:T(1,128)S(1)} %bitcast.2, ...), custom_call_target="tpu_custom_call" | custom-call | flops 1000000000 | bytes 1000000 | tf_op jit(solution)/shard_map/weights/pallas_call | solution.py:426
  9.8 0.0 collective-permute-done.lo_ref
  9.8 2.2 %collective-permute-done.1.hi_ref = bf16[120,256]{1,0:T(8,128)(2,1)S(1)} collective-permute-done((bf16[120,256]{1,0:T(8,128)(2,1)}, bf16[120,256]{1,0:T(8,128)(2,1)S(1)}, u32[]{:S(2)}, u32[]{:S(2)}) %collective-permute-start.1) | collective-permute-done | bytes 61472 | tf_op jit(solution)/shard_map/ppermute | solution.py:424
  12.0 0.0 copy-done
  12.0 0.0 copy-done.1
  12.0 26.2 %align.1 = f32[3,2,128,128]{3,2,1,0:T(8,128)} custom-call(s32[3]{0:T(128)S(1)} %broadcast_add_fusion.chain_ref, bf16[4,256,256]{2,1,0:T(8,128)(2,1)S(1)} %copy-done, bf16[120,256]{1,0:T(8,128)(2,1)S(1)} %collective-permute-done.lo_ref, bf16[120,256]{1,0:T(8,128)(2,1)S(1)} %collective-permute-done.1.hi_ref, f32[2,128,128]{2,1,0:T(8,128)S(1)} %copy-done.1, ...), custom_call_target="tpu_custom_call" | custom-call | tf_op jit(solution)/shard_map/align/pallas_call | solution.py:442
  (1 shorter events, 0.0 us)
Async XLA Ops:
  0.0 7.4 %copy-start.2 = (bf16[9,32,32]{2,1,0:T(8,128)(2,1)S(1)}, bf16[9,32,32]{2,1,0:T(8,128)(2,1)}, u32[]{:S(2)}) copy-start(bf16[9,32,32]{2,1,0:T(8,128)(2,1)} %c2_ref.1) | copy-start | bytes 55300
  0.0 7.3 %copy-start.7 = (s32[3]{0:T(128)S(1)}, s32[3]{0:T(128)}, u32[]{:S(2)}) copy-start(s32[3]{0:T(128)} %param.9) | copy-start | bytes 40
  1.6 5.7 %copy-start.6 = (bf16[32,9]{0,1:T(8,128)(2,1)S(1)}, bf16[32,9]{0,1:T(8,128)(2,1)}, u32[]{:S(2)}) copy-start(bf16[32,9]{0,1:T(8,128)(2,1)} %param.11) | copy-start | bytes 1732
  1.6 8.1 %collective-permute-start = (bf16[120,256]{1,0:T(8,128)(2,1)}, bf16[120,256]{1,0:T(8,128)(2,1)S(1)}, u32[]{:S(2)}, u32[]{:S(2)}) collective-permute-start(bf16[120,256]{1,0:T(8,128)(2,1)} %get-tuple-element.10), channel_id=1, source_target_pairs={{0,1},{1,2},{2,3},{3,4},{4,5},{5,6},{6,7},{7,8},{8,9},{9,10},{10,1... | collective-permute-start | bytes 184328 | tf_op jit(solution)/shard_map/ppermute | solution.py:423
  5.3 6.6 %collective-permute-start.1 = (bf16[120,256]{1,0:T(8,128)(2,1)}, bf16[120,256]{1,0:T(8,128)(2,1)S(1)}, u32[]{:S(2)}, u32[]{:S(2)}) collective-permute-start(bf16[120,256]{1,0:T(8,128)(2,1)} %get-tuple-element.11), channel_id=1, source_target_pairs={{1,0},{2,1},{3,2},{4,3},{5,4},{6,5},{7,6},{8,7},{9,8},{10,9},{11,1... | collective-permute-start | bytes 184328 | tf_op jit(solution)/shard_map/ppermute | solution.py:424
  7.4 0.7 %copy-start.3 = (f32[32]{0:T(128)S(1)}, f32[32]{0:T(128)}, u32[]{:S(2)}) copy-start(f32[32]{0:T(128)} %param.12) | copy-start | bytes 388
  7.4 0.7 %copy-start.4 = (f32[32]{0:T(128)S(1)}, f32[32]{0:T(128)}, u32[]{:S(2)}) copy-start(f32[32]{0:T(128)} %param.14) | copy-start | bytes 388
  7.4 0.7 %copy-start.5 = (s32[1,128]{1,0:T(1,128)S(1)}, s32[1,128]{1,0:T(1,128)}, u32[]{:S(2)}) copy-start(s32[1,128]{1,0:T(1,128)} %constant.4.clone.lanes_ref) | copy-start | bytes 1540
  8.1 3.9 %copy-start = (bf16[4,256,256]{2,1,0:T(8,128)(2,1)S(1)}, bf16[4,256,256]{2,1,0:T(8,128)(2,1)}, u32[]{:S(2)}) copy-start(bf16[4,256,256]{2,1,0:T(8,128)(2,1)} %img_ref.3) | copy-start | bytes 1572868
  8.1 3.9 %copy-start.1 = (f32[2,128,128]{2,1,0:T(8,128)S(1)}, f32[2,128,128]{2,1,0:T(8,128)}, u32[]{:S(2)}) copy-start(f32[2,128,128]{2,1,0:T(8,128)} %fld_ref.3) | copy-start | bytes 393220

commit v4 on v3

--- a/solution.py
+++ b/solution.py
@@ -132,9 +132,9 @@
 def kernel(
     sections, rows, total_rows, channels,
     chain_ref, img_ref, lo_ref, hi_ref, fld_ref, w1_ref, w2_ref, b2_ref,
-    out_ref, z_ref, x_ref, p0_ref, p1_ref, t_ref, f_ref, s0_ref, s1_ref,
+    out_ref, z_ref, x_ref, a0_ref, a1_ref, b0_ref, b1_ref, t_ref, f_ref, s0_ref, s1_ref,
 ):
-    groups = p0_ref.shape[1]
+    groups = a0_ref.shape[1]
     span = x_ref.shape[0] // groups
     per = LANES // channels
     lane = lane_index((1, LANES))
@@ -171,7 +171,9 @@
                     first[half * odd : half * (odd + 1)], w2_ref[part + 2 * odd], preferred_element_type=jnp.float32
                 )
                 at = groups // 2 * odd
-                target[part, at : at + groups // 2, PAD : PAD + span, :] = second.reshape(groups // 2, span, WIDE)
+                second = second.reshape(groups // 2, span, WIDE)
+                target[0][part, at : at + groups // 2, PAD : PAD + span, :] = second[:, :, :LANES]
+                target[1][part, at : at + groups // 2] = second[:, :, LANES:]
 
     def features(k, xh, source):
         valid = inside_mask(k)
@@ -180,10 +182,10 @@
                 parts = []
                 for q in range(per):
                     part, odd = q % 2, q // 2
-                    at = (source, part, 2 * side + half + 4 * odd)
-                    above = at[0][at[1], at[2], PAD - 1 : PAD - 1 + span, 0:LANES]
-                    below = at[0][at[1], at[2], PAD + 1 : PAD + 1 + span, 0:LANES]
-                    here = at[0][at[1], at[2], PAD : PAD + span, LANES:WIDE]
+                    at = 2 * side + half + 4 * odd
+                    above = source[0][part, at, PAD - 1 : PAD - 1 + span, :]
+                    below = source[0][part, at, PAD + 1 : PAD + 1 + span, :]
+                    here = source[1][part, at]
                     summed = here + jnp.where((slot + per - q) % per < 2, above, below)
                     parts.append(jnp.tanh(summed + b2_ref[0:1, :]) * valid)
                 for t in range(per):
@@ -254,14 +256,14 @@
             x_ref[pl.ds(span * at, span), 0:LANES] = left * valid.astype(jnp.bfloat16)
             x_ref[pl.ds(span * at, span), LANES:WIDE] = right * valid.astype(jnp.bfloat16)
 
-        buffers = (p0_ref, p1_ref)
+        buffers = ((a0_ref, b0_ref), (a1_ref, b1_ref))
         for xh in range(4):
             layers(xh, buffers[xh % 2])
             features(k if xh else jnp.maximum(k - 1, 0), (xh - 1) % 4, buffers[(xh - 1) % 2])
         return carry
 
     lax.fori_loop(0, sections + 1, encode, 0)
-    features(sections, 3, p1_ref)
+    features(sections, 3, (a1_ref, b1_ref))
 
     scale = SHARPNESS / channels * math.log2(math.e)
     sub8 = lax.broadcasted_iota(jnp.int32, (8, LANES), 0)
@@ -273,6 +275,7 @@
     row_weight = row_at.astype(jnp.float32)
     row_mask = jnp.where((row_at >= y_of) & (row_at <= y_of + 2 * REACH), 1.0, 0.0)
     pick = channels * ((lane8 // 8) % 4) + 8 * (lane8 % 4) + 4 * (sub8 % 2) + sub8 // 2
+    beyond = [jnp.where(x_of > m, 9.0, 0.0) for m in range(3)]
     patch = [jnp.where(slot == q, 1.0, 0.0).astype(jnp.bfloat16) for q in range(per)]
 
     def gather(values, index):
@@ -291,35 +294,41 @@
             first = jnp.where(t >= starts[n], starts[n], first)
         return k, 2 * (t - first)
 
-    def scores(k, i, side, h):
-        lhs, rhs = [], []
+    def scores(k, i, side):
+        lhs, rhs = [], [[], []]
         for half in range(2):
-            window = t_ref[k - 1, 4 * h : 4 * h + 12, :, side, half, pl.ds(PAD + 1 + 4 * i, 8), :]
-            lhs.append(window.reshape(12 * 16, LANES).astype(jnp.bfloat16))
-            even = t_ref[k, 4 + 4 * h : 8 + 4 * h, 0, side, half, pl.ds(PAD + 1 + 4 * i, 8), :]
-            odd = t_ref[k, 4 + 4 * h : 8 + 4 * h, 1, side, half, pl.ds(PAD - 3 + 4 * i, 8), :]
+            window = t_ref[k - 1, :, :, side, half, pl.ds(PAD + 1 + 4 * i, 8), :]
+            lhs.append(window.reshape(16 * 16, LANES).astype(jnp.bfloat16))
+            even = t_ref[k, 4:12, 0, side, half, pl.ds(PAD + 1 + 4 * i, 8), :]
+            odd = t_ref[k, 4:12, 1, side, half, pl.ds(PAD - 3 + 4 * i, 8), :]
             current = jnp.where(sub8 < 4, even, odd) * scale
-            current = current.reshape(32, LANES).astype(jnp.bfloat16)
-            nothing = jnp.zeros_like(current)
-            for q in range(per):
-                masked = current * patch[q]
-                rhs.append(jnp.concatenate([masked, nothing] if half == 0 else [nothing, masked], axis=1))
+            current = current.reshape(64, LANES).astype(jnp.bfloat16)
+            for h in range(2):
+                mine = current[32 * h : 32 * (h + 1)]
+                nothing = jnp.zeros_like(mine)
+                for q in range(per):
+                    masked = mine * patch[q]
+                    rhs[h].append(jnp.concatenate([masked, nothing] if half == 0 else [nothing, masked], axis=1))
         lhs = jnp.concatenate(lhs, axis=1)
-        rhs = jnp.concatenate(rhs, axis=0)
-        return lax.dot_general(lhs, rhs, (((1,), (1,)), ((), ())), preferred_element_type=jnp.float32)
+        return [
+            lax.dot_general(
+                lhs[64 * h : 64 * h + 192], jnp.concatenate(rhs[h], axis=0), (((1,), (1,)), ((), ())),
+                preferred_element_type=jnp.float32,
+            )
+            for h in range(2)
+        ]
 
     def means(source, at):
-        running = jnp.zeros((2, 8, WIDE), jnp.float32)
-        moment = jnp.zeros((2, 8, WIDE), jnp.float32)
-        for u in range(11, -1, -1):
-            term = jnp.exp2(source[at, 16 * u : 16 * u + 16, :]).reshape(2, 8, WIDE)
-            if u < 3:
-                term = jnp.where(x_of <= u, term, 0.0)
-            if u > 8:
-                term = jnp.where(x_of >= u - 8, term, 0.0)
-            running = running + term
-            if u:
-                moment = moment + running
+        for m in range(8, -1, -1):
+            score = source[at, 16 * m : 16 * m + 16, :]
+            if m < 3:
+                score = jnp.where(x_of <= m, score, source[at, 16 * m + 144 : 16 * m + 160, :])
+            term = jnp.exp2(score).reshape(2, 8, WIDE)
+            running = running + term if m < 8 else term
+            if m:
+                moment = moment + running if m < 8 else running
+            if m < 3:
+                moment = moment + term * beyond[m]
         running = running * row_mask
         moment = moment * row_mask
         total = jnp.sum(running[0] + running[1], axis=0, keepdims=True)
@@ -350,9 +359,9 @@
         inside = (row >= 0) & (row < total_rows)
         return [jnp.where(inside, value, 0.0) for value in sums]
 
-    def fill(t, target, at):
+    def fill(t, target, n, side):
         k, i = place(t)
-        target[at] = scores(k, i + at // 4, at // 2 % 2, at % 2)
+        target[4 * n + 2 * side], target[4 * n + 2 * side + 1] = scores(k, i + n, side)
 
     def finish(t, found):
         k, i = place(t)
@@ -367,9 +376,9 @@
             down = jnp.zeros((8, LANES), jnp.float32)
             across = jnp.zeros((8, LANES), jnp.float32)
             for side in range(2):
+                fill(t + 1, target, n, side)
                 for h in range(2):
                     at = 4 * n + 2 * side + h
-                    fill(t + 1, target, at)
                     y_mean, x_mean = means(source, at)
                     for half in range(2):
                         keep = (lane8 // 64 == side) & ((lane8 // 32) % 2 == half) & ((lane8 // 4) % 2 == h)
@@ -385,8 +394,8 @@
         carry = step(2 * j, carry, s0_ref, s1_ref)
         return step(2 * j + 1, carry, s1_ref, s0_ref)
 
-    for at in range(8):
-        fill(0, s0_ref, at)
+    for at in range(4):
+        fill(0, s0_ref, at // 2, at % 2)
     turns = pl.cdiv(blocks, 2)
     found = lax.fori_loop(0, turns, two_steps, (jnp.zeros((8, LANES), jnp.float32),) * 4)
     finish(2 * turns - 1, found)
@@ -447,8 +456,10 @@
         scratch_shapes=[
             pltpu.VMEM((2, 2 * rows + 96, LANES), jnp.float32),
             pltpu.VMEM((groups * span, WIDE), jnp.bfloat16),
-            pltpu.VMEM((2, groups, span + 2 * PAD, WIDE), jnp.float32),
-            pltpu.VMEM((2, groups, span + 2 * PAD, WIDE), jnp.float32),
+            pltpu.VMEM((2, groups, span + 2 * PAD, LANES), jnp.float32),
+            pltpu.VMEM((2, groups, span + 2 * PAD, LANES), jnp.float32),
+            pltpu.VMEM((2, groups, span, LANES), jnp.float32),
+            pltpu.VMEM((2, groups, span, LANES), jnp.float32),
             pltpu.VMEM((sections + 1, 16, 2, 2, 2, span + 2 * PAD, LANES), jnp.float32),
             pltpu.VMEM((sections + 1, 2, rows + 2 * FIELD_HALO + 8, LANES), jnp.float32),
             pltpu.VMEM((8, 192, WIDE), jnp.float32),

time: 38.5 us -> 37.6 us (0.977)
  Pallas kernels: 29.5 us -> 28.6 us
    pallas_call x1, Pallas kernels: 26.2 us -> 25.3 us  [on_device(): pl.pallas_call(functools.partial(kernel, sections, rows, rows * count, ch...]
where the time goes in v4:
time: 37.6 us; the launch traced here: 37.3 us
  Pallas kernels  28.6 us (76%)
  starting transfers between devices  5.63 us (15%)
  waiting for transfers between devices  2.23 us (6%)
  local copies, waits for them, and re-layouts  0.79 us (2%)
    pallas_call x1, Pallas kernels, on_device(): pl.pallas_call(functools.partial(kernel, sections, rows, rows * count, ch...  25.3 us
    ppermute x1, starting transfers between devices, on_device(): lo = lax.ppermute(up, 'tile', forward)  3.71 us
    ppermute x1, waiting for transfers between devices, on_device(): hi = lax.ppermute(down, 'tile', backward)  2.23 us
    ppermute x1, starting transfers between devices, on_device(): hi = lax.ppermute(down, 'tile', backward)  1.92 us
    pallas_call x1, Pallas kernels, on_device(): pl.pallas_call(prepare, out_shape=(jax.ShapeDtypeStruct((WINDOWS, WIDE, W...  1.65 us
    pallas_call x1, Pallas kernels, on_device(): pl.pallas_call(pack, out_shape=(jax.ShapeDtypeStruct((held, columns), ima...  1.6 us
    unnamed x17, local copies, waits for them, and re-layouts  0.79 us
  transfers between devices with their start and end apart: 2, of which 1 were waited for; matrix products, arithmetic and copies ran while one was open for 0% of the time, Pallas kernels for 4%

profile of v4, /device:TPU:21, one launch (start us, length us, event | category | flops | bytes accessed | tf_op | source)
XLA Modules:
  0.0 37.3 jit_solution(6632971873983850436)
XLA Ops:
  0.0 0.0 copy-start.2
  0.0 0.0 copy-start.7
  0.0 1.6 %pack.1 = (bf16[120,256]{1,0:T(8,128)(2,1)}, bf16[120,256]{1,0:T(8,128)(2,1)}) custom-call(bf16[4,256,256]{2,1,0:T(8,128)(2,1)} %img_ref.3, f32[2,128,128]{2,1,0:T(8,128)} %fld_ref.3), custom_call_target="tpu_custom_call" | custom-call | tf_op jit(solution)/shard_map/pack/pallas_call | solution.py:419
  1.6 0.0 copy-start.6
  1.6 3.7 %collective-permute-start = (bf16[120,256]{1,0:T(8,128)(2,1)}, bf16[120,256]{1,0:T(8,128)(2,1)S(1)}, u32[]{:S(2)}, u32[]{:S(2)}) collective-permute-start(bf16[120,256]{1,0:T(8,128)(2,1)} %get-tuple-element.10), channel_id=1, source_target_pairs={{0,1},{1,2},{2,3},{3,4},{4,5},{5,6},{6,7},{7,8},{8,9},{9,10},{10,1... | collective-permute-start | bytes 184328 | tf_op jit(solution)/shard_map/ppermute | solution.py:432
  5.3 1.9 %collective-permute-start.1 = (bf16[120,256]{1,0:T(8,128)(2,1)}, bf16[120,256]{1,0:T(8,128)(2,1)S(1)}, u32[]{:S(2)}, u32[]{:S(2)}) collective-permute-start(bf16[120,256]{1,0:T(8,128)(2,1)} %get-tuple-element.11), channel_id=1, source_target_pairs={{1,0},{2,1},{3,2},{4,3},{5,4},{6,5},{7,6},{8,7},{9,8},{10,9},{11,1... | collective-permute-start | bytes 184328 | tf_op jit(solution)/shard_map/ppermute | solution.py:433
  7.3 0.0 copy-done.7
  7.3 0.0 copy-done.6
  7.3 0.1 copy.9.c1_ref
  7.4 0.0 copy-start.3
  7.4 0.0 copy-start.4
  7.4 0.0 copy-start.5
  7.4 0.0 copy-done.2
  7.4 0.6 %copy-done.3 = f32[32]{0:T(128)S(1)} copy-done((f32[32]{0:T(128)S(1)}, f32[32]{0:T(128)}, u32[]{:S(2)}) %copy-start.3) | copy-done | bytes 152
  8.1 0.0 copy-done.4
  8.1 0.0 copy-done.5
  8.1 0.0 copy-start
  8.1 0.0 copy-start.1
  8.1 1.7 %weights.1 = (bf16[8,256,256]{2,1,0:T(8,128)(2,1)S(1)}, bf16[4,256,256]{2,1,0:T(8,128)(2,1)S(1)}, f32[8,128]{1,0:T(8,128)S(1)}) custom-call(s32[3]{0:T(128)S(1)} %broadcast_add_fusion.chain_ref, s32[1,128]{1,0:T(1,128)S(1)} %copy-done.5, bf16[32,9]{1,0:T(8,128)(2,1)S(1)} %copy.9.c1_ref, f32[1,32]{1,0:T(1,128)S(1)} %bitcast.2, ...), custom_call_target="tpu_custom_call" | custom-call | flops 1000000000 | bytes 1000000 | tf_op jit(solution)/shard_map/weights/pallas_call | solution.py:435
  9.8 0.0 collective-permute-done.lo_ref
  9.8 2.2 %collective-permute-done.1.hi_ref = bf16[120,256]{1,0:T(8,128)(2,1)S(1)} collective-permute-done((bf16[120,256]{1,0:T(8,128)(2,1)}, bf16[120,256]{1,0:T(8,128)(2,1)S(1)}, u32[]{:S(2)}, u32[]{:S(2)}) %collective-permute-start.1) | collective-permute-done | bytes 61472 | tf_op jit(solution)/shard_map/ppermute | solution.py:433
  12.0 0.0 copy-done
  12.0 0.0 copy-done.1
  12.0 25.3 %align.1 = f32[3,2,128,128]{3,2,1,0:T(8,128)} custom-call(s32[3]{0:T(128)S(1)} %broadcast_add_fusion.chain_ref, bf16[4,256,256]{2,1,0:T(8,128)(2,1)S(1)} %copy-done, bf16[120,256]{1,0:T(8,128)(2,1)S(1)} %collective-permute-done.lo_ref, bf16[120,256]{1,0:T(8,128)(2,1)S(1)} %collective-permute-done.1.hi_ref, f32[2,128,128]{2,1,0:T(8,128)S(1)} %copy-done.1, ...), custom_call_target="tpu_custom_call" | custom-call | tf_op jit(solution)/shard_map/align/pallas_call | solution.py:451
  (1 shorter events, 0.0 us)
Async XLA Ops:
  0.0 7.4 %copy-start.2 = (bf16[9,32,32]{2,1,0:T(8,128)(2,1)S(1)}, bf16[9,32,32]{2,1,0:T(8,128)(2,1)}, u32[]{:S(2)}) copy-start(bf16[9,32,32]{2,1,0:T(8,128)(2,1)} %c2_ref.1) | copy-start | bytes 55300
  0.0 7.3 %copy-start.7 = (s32[3]{0:T(128)S(1)}, s32[3]{0:T(128)}, u32[]{:S(2)}) copy-start(s32[3]{0:T(128)} %param.9) | copy-start | bytes 40
  1.6 5.7 %copy-start.6 = (bf16[32,9]{0,1:T(8,128)(2,1)S(1)}, bf16[32,9]{0,1:T(8,128)(2,1)}, u32[]{:S(2)}) copy-start(bf16[32,9]{0,1:T(8,128)(2,1)} %param.11) | copy-start | bytes 1732
  1.6 8.1 %collective-permute-start = (bf16[120,256]{1,0:T(8,128)(2,1)}, bf16[120,256]{1,0:T(8,128)(2,1)S(1)}, u32[]{:S(2)}, u32[]{:S(2)}) collective-permute-start(bf16[120,256]{1,0:T(8,128)(2,1)} %get-tuple-element.10), channel_id=1, source_target_pairs={{0,1},{1,2},{2,3},{3,4},{4,5},{5,6},{6,7},{7,8},{8,9},{9,10},{10,1... | collective-permute-start | bytes 184328 | tf_op jit(solution)/shard_map/ppermute | solution.py:432
  5.3 6.6 %collective-permute-start.1 = (bf16[120,256]{1,0:T(8,128)(2,1)}, bf16[120,256]{1,0:T(8,128)(2,1)S(1)}, u32[]{:S(2)}, u32[]{:S(2)}) collective-permute-start(bf16[120,256]{1,0:T(8,128)(2,1)} %get-tuple-element.11), channel_id=1, source_target_pairs={{1,0},{2,1},{3,2},{4,3},{5,4},{6,5},{7,6},{8,7},{9,8},{10,9},{11,1... | collective-permute-start | bytes 184328 | tf_op jit(solution)/shard_map/ppermute | solution.py:433
  7.4 0.7 %copy-start.3 = (f32[32]{0:T(128)S(1)}, f32[32]{0:T(128)}, u32[]{:S(2)}) copy-start(f32[32]{0:T(128)} %param.12) | copy-start | bytes 388
  7.4 0.7 %copy-start.4 = (f32[32]{0:T(128)S(1)}, f32[32]{0:T(128)}, u32[]{:S(2)}) copy-start(f32[32]{0:T(128)} %param.14) | copy-start | bytes 388
  7.4 0.7 %copy-start.5 = (s32[1,128]{1,0:T(1,128)S(1)}, s32[1,128]{1,0:T(1,128)}, u32[]{:S(2)}) copy-start(s32[1,128]{1,0:T(1,128)} %constant.4.clone.lanes_ref) | copy-start | bytes 1540
  8.1 3.9 %copy-start = (bf16[4,256,256]{2,1,0:T(8,128)(2,1)S(1)}, bf16[4,256,256]{2,1,0:T(8,128)(2,1)}, u32[]{:S(2)}) copy-start(bf16[4,256,256]{2,1,0:T(8,128)(2,1)} %img_ref.3) | copy-start | bytes 1572868
  8.1 3.9 %copy-start.1 = (f32[2,128,128]{2,1,0:T(8,128)S(1)}, f32[2,128,128]{2,1,0:T(8,128)}, u32[]{:S(2)}) copy-start(f32[2,128,128]{2,1,0:T(8,128)} %fld_ref.3) | copy-start | bytes 393220

commit v5 on v4

--- a/solution.py
+++ b/solution.py
@@ -135,7 +135,7 @@
     out_ref, z_ref, x_ref, a0_ref, a1_ref, b0_ref, b1_ref, t_ref, f_ref, s0_ref, s1_ref,
 ):
     groups = a0_ref.shape[1]
-    span = x_ref.shape[0] // groups
+    largest = x_ref.shape[0] // groups
     per = LANES // channels
     lane = lane_index((1, LANES))
     slot = lane // channels
@@ -150,14 +150,14 @@
             part = ref[pictures : pictures + FIELD_HALO, LANES * c : LANES * (c + 1)]
             f_ref[0, c, start : start + FIELD_HALO, :] = part.astype(jnp.float32)
 
-    def inside_mask(k):
+    def inside_mask(k, span):
         pair = lax.broadcasted_iota(jnp.int32, (span, LANES), 0) + tile * (rows // 2) - 1
         pair = pair - REACH * (sections - k) // 2
         return jnp.where((pair >= 0) & (pair < pairs_total), 1.0, 0.0)
 
-    def layers(xh, target):
+    def layers(xh, target, span):
         for part in range(2):
-            first = jnp.dot(x_ref[...], w1_ref[xh + 4 * part], preferred_element_type=jnp.float32)
+            first = jnp.dot(x_ref[: groups * span], w1_ref[xh + 4 * part], preferred_element_type=jnp.float32)
             first = jnp.maximum(first, 0.0)
             edge = (lane_index((1, WIDE)) // channels) % 4
             if xh == 0 and part == 0:
@@ -173,10 +173,10 @@
                 at = groups // 2 * odd
                 second = second.reshape(groups // 2, span, WIDE)
                 target[0][part, at : at + groups // 2, PAD : PAD + span, :] = second[:, :, :LANES]
-                target[1][part, at : at + groups // 2] = second[:, :, LANES:]
-
-    def features(k, xh, source):
-        valid = inside_mask(k)
+                target[1][part, at : at + groups // 2, 0:span, :] = second[:, :, LANES:]
+
+    def features(k, xh, source, span):
+        valid = inside_mask(k, span)
         for side in range(2):
             for half in range(2):
                 parts = []
@@ -185,7 +185,7 @@
                     at = 2 * side + half + 4 * odd
                     above = source[0][part, at, PAD - 1 : PAD - 1 + span, :]
                     below = source[0][part, at, PAD + 1 : PAD + 1 + span, :]
-                    here = source[1][part, at]
+                    here = source[1][part, at, 0:span, :]
                     summed = here + jnp.where((slot + per - q) % per < 2, above, below)
                     parts.append(jnp.tanh(summed + b2_ref[0:1, :]) * valid)
                 for t in range(per):
@@ -213,7 +213,7 @@
                     else:
                         own[...] = jnp.where(slot == edge, 0.0, moved)
 
-    def encode(k, carry):
+    def encode(span, before, k, carry):
         extra = REACH * (sections - k)
         section = jnp.where(k == 0, 0, chain_ref[jnp.maximum(k - 1, 0)])
         first = jnp.where(k == 0, 0, HALO + LATER * (section - 1))
@@ -234,7 +234,7 @@
                 z_ref[half, pl.ds(base - HALO, far), :] = lo_ref[0:far, cols].astype(jnp.float32)
                 z_ref[half, pl.ds(base + 2 * rows + LATER, far), :] = hi_ref[LATER:HALO, cols].astype(jnp.float32)
 
-        valid = inside_mask(k)
+        valid = inside_mask(k, span)
         for group in range(groups):
             side, place = divmod(group, groups // 2)
             at = group // 2 + groups // 2 * (group % 2)
@@ -258,12 +258,20 @@
 
         buffers = ((a0_ref, b0_ref), (a1_ref, b1_ref))
         for xh in range(4):
-            layers(xh, buffers[xh % 2])
-            features(k if xh else jnp.maximum(k - 1, 0), (xh - 1) % 4, buffers[(xh - 1) % 2])
+            layers(xh, buffers[xh % 2], span)
+            last = buffers[(xh - 1) % 2]
+            if xh:
+                features(k, xh - 1, last, span)
+            else:
+                features(jnp.maximum(k - 1, 0), 3, last, before)
         return carry
 
-    lax.fori_loop(0, sections + 1, encode, 0)
-    features(sections, 3, (a1_ref, b1_ref))
+    half = (sections + 1) // 2
+    fewer = pl.cdiv((rows + 2 * REACH * (sections - half)) // 2 + 2, 8) * 8
+    lax.fori_loop(0, half, functools.partial(encode, largest, largest), 0)
+    encode(fewer, largest, half, 0)
+    lax.fori_loop(half + 1, sections + 1, functools.partial(encode, fewer, fewer), 0)
+    features(sections, 3, (a1_ref, b1_ref), fewer)
 
     scale = SHARPNESS / channels * math.log2(math.e)
     sub8 = lax.broadcasted_iota(jnp.int32, (8, LANES), 0)

time: 37.6 us -> 37.3 us (level)
  no operation moved by 1% of the time
where the time goes in v5:
time: 37.3 us; the launch traced here: 37.1 us
  Pallas kernels  28.4 us (76%)
  starting transfers between devices  5.63 us (15%)
  waiting for transfers between devices  2.23 us (6%)
  local copies, waits for them, and re-layouts  0.79 us (2%)
    pallas_call x1, Pallas kernels, on_device(): pl.pallas_call(functools.partial(kernel, sections, rows, rows * count, ch...  25.1 us
    ppermute x1, starting transfers between devices, on_device(): lo = lax.ppermute(up, 'tile', forward)  3.71 us
    ppermute x1, waiting for transfers between devices, on_device(): hi = lax.ppermute(down, 'tile', backward)  2.23 us
    ppermute x1, starting transfers between devices, on_device(): hi = lax.ppermute(down, 'tile', backward)  1.92 us
    pallas_call x1, Pallas kernels, on_device(): pl.pallas_call(prepare, out_shape=(jax.ShapeDtypeStruct((WINDOWS, WIDE, W...  1.65 us
    pallas_call x1, Pallas kernels, on_device(): pl.pallas_call(pack, out_shape=(jax.ShapeDtypeStruct((held, columns), ima...  1.6 us
    unnamed x17, local copies, waits for them, and re-layouts  0.79 us
  transfers between devices with their start and end apart: 2, of which 1 were waited for; matrix products, arithmetic and copies ran while one was open for 0% of the time, Pallas kernels for 4%

profile of v5, /device:TPU:21, one launch (start us, length us, event | category | flops | bytes accessed | tf_op | source)
XLA Modules:
  0.0 37.1 jit_solution(16020337801504153153)
XLA Ops:
  0.0 0.0 copy-start.2
  0.0 0.0 copy-start.7
  0.0 1.6 %pack.1 = (bf16[120,256]{1,0:T(8,128)(2,1)}, bf16[120,256]{1,0:T(8,128)(2,1)}) custom-call(bf16[4,256,256]{2,1,0:T(8,128)(2,1)} %img_ref.3, f32[2,128,128]{2,1,0:T(8,128)} %fld_ref.3), custom_call_target="tpu_custom_call" | custom-call | tf_op jit(solution)/shard_map/pack/pallas_call | solution.py:427
  1.6 0.0 copy-start.6
  1.6 3.7 %collective-permute-start = (bf16[120,256]{1,0:T(8,128)(2,1)}, bf16[120,256]{1,0:T(8,128)(2,1)S(1)}, u32[]{:S(2)}, u32[]{:S(2)}) collective-permute-start(bf16[120,256]{1,0:T(8,128)(2,1)} %get-tuple-element.10), channel_id=1, source_target_pairs={{0,1},{1,2},{2,3},{3,4},{4,5},{5,6},{6,7},{7,8},{8,9},{9,10},{10,1... | collective-permute-start | bytes 184328 | tf_op jit(solution)/shard_map/ppermute | solution.py:440
  5.3 1.9 %collective-permute-start.1 = (bf16[120,256]{1,0:T(8,128)(2,1)}, bf16[120,256]{1,0:T(8,128)(2,1)S(1)}, u32[]{:S(2)}, u32[]{:S(2)}) collective-permute-start(bf16[120,256]{1,0:T(8,128)(2,1)} %get-tuple-element.11), channel_id=1, source_target_pairs={{1,0},{2,1},{3,2},{4,3},{5,4},{6,5},{7,6},{8,7},{9,8},{10,9},{11,1... | collective-permute-start | bytes 184328 | tf_op jit(solution)/shard_map/ppermute | solution.py:441
  7.3 0.0 copy-done.7
  7.3 0.0 copy-done.6
  7.3 0.1 copy.9.c1_ref
  7.4 0.0 copy-start.3
  7.4 0.0 copy-start.4
  7.4 0.0 copy-start.5
  7.4 0.0 copy-done.2
  7.4 0.6 %copy-done.3 = f32[32]{0:T(128)S(1)} copy-done((f32[32]{0:T(128)S(1)}, f32[32]{0:T(128)}, u32[]{:S(2)}) %copy-start.3) | copy-done | bytes 152
  8.1 0.0 copy-done.4
  8.1 0.0 copy-done.5
  8.1 0.0 copy-start
  8.1 0.0 copy-start.1
  8.1 1.7 %weights.1 = (bf16[8,256,256]{2,1,0:T(8,128)(2,1)S(1)}, bf16[4,256,256]{2,1,0:T(8,128)(2,1)S(1)}, f32[8,128]{1,0:T(8,128)S(1)}) custom-call(s32[3]{0:T(128)S(1)} %broadcast_add_fusion.chain_ref, s32[1,128]{1,0:T(1,128)S(1)} %copy-done.5, bf16[32,9]{1,0:T(8,128)(2,1)S(1)} %copy.9.c1_ref, f32[1,32]{1,0:T(1,128)S(1)} %bitcast.2, ...), custom_call_target="tpu_custom_call" | custom-call | flops 1000000000 | bytes 1000000 | tf_op jit(solution)/shard_map/weights/pallas_call | solution.py:443
  9.8 0.0 collective-permute-done.lo_ref
  9.8 2.2 %collective-permute-done.1.hi_ref = bf16[120,256]{1,0:T(8,128)(2,1)S(1)} collective-permute-done((bf16[120,256]{1,0:T(8,128)(2,1)}, bf16[120,256]{1,0:T(8,128)(2,1)S(1)}, u32[]{:S(2)}, u32[]{:S(2)}) %collective-permute-start.1) | collective-permute-done | bytes 61472 | tf_op jit(solution)/shard_map/ppermute | solution.py:441
  12.0 0.0 copy-done
  12.0 0.0 copy-done.1
  12.0 25.1 %align.1 = f32[3,2,128,128]{3,2,1,0:T(8,128)} custom-call(s32[3]{0:T(128)S(1)} %broadcast_add_fusion.chain_ref, bf16[4,256,256]{2,1,0:T(8,128)(2,1)S(1)} %copy-done, bf16[120,256]{1,0:T(8,128)(2,1)S(1)} %collective-permute-done.lo_ref, bf16[120,256]{1,0:T(8,128)(2,1)S(1)} %collective-permute-done.1.hi_ref, f32[2,128,128]{2,1,0:T(8,128)S(1)} %copy-done.1, ...), custom_call_target="tpu_custom_call" | custom-call | tf_op jit(solution)/shard_map/align/pallas_call | solution.py:459
  (1 shorter events, 0.0 us)
Async XLA Ops:
  0.0 7.4 %copy-start.2 = (bf16[9,32,32]{2,1,0:T(8,128)(2,1)S(1)}, bf16[9,32,32]{2,1,0:T(8,128)(2,1)}, u32[]{:S(2)}) copy-start(bf16[9,32,32]{2,1,0:T(8,128)(2,1)} %c2_ref.1) | copy-start | bytes 55300
  0.0 7.3 %copy-start.7 = (s32[3]{0:T(128)S(1)}, s32[3]{0:T(128)}, u32[]{:S(2)}) copy-start(s32[3]{0:T(128)} %param.9) | copy-start | bytes 40
  1.6 5.7 %copy-start.6 = (bf16[32,9]{0,1:T(8,128)(2,1)S(1)}, bf16[32,9]{0,1:T(8,128)(2,1)}, u32[]{:S(2)}) copy-start(bf16[32,9]{0,1:T(8,128)(2,1)} %param.11) | copy-start | bytes 1732
  1.6 8.1 %collective-permute-start = (bf16[120,256]{1,0:T(8,128)(2,1)}, bf16[120,256]{1,0:T(8,128)(2,1)S(1)}, u32[]{:S(2)}, u32[]{:S(2)}) collective-permute-start(bf16[120,256]{1,0:T(8,128)(2,1)} %get-tuple-element.10), channel_id=1, source_target_pairs={{0,1},{1,2},{2,3},{3,4},{4,5},{5,6},{6,7},{7,8},{8,9},{9,10},{10,1... | collective-permute-start | bytes 184328 | tf_op jit(solution)/shard_map/ppermute | solution.py:440
  5.3 6.6 %collective-permute-start.1 = (bf16[120,256]{1,0:T(8,128)(2,1)}, bf16[120,256]{1,0:T(8,128)(2,1)S(1)}, u32[]{:S(2)}, u32[]{:S(2)}) collective-permute-start(bf16[120,256]{1,0:T(8,128)(2,1)} %get-tuple-element.11), channel_id=1, source_target_pairs={{1,0},{2,1},{3,2},{4,3},{5,4},{6,5},{7,6},{8,7},{9,8},{10,9},{11,1... | collective-permute-start | bytes 184328 | tf_op jit(solution)/shard_map/ppermute | solution.py:441
  7.4 0.7 %copy-start.3 = (f32[32]{0:T(128)S(1)}, f32[32]{0:T(128)}, u32[]{:S(2)}) copy-start(f32[32]{0:T(128)} %param.12) | copy-start | bytes 388
  7.4 0.7 %copy-start.4 = (f32[32]{0:T(128)S(1)}, f32[32]{0:T(128)}, u32[]{:S(2)}) copy-start(f32[32]{0:T(128)} %param.14) | copy-start | bytes 388
  7.4 0.7 %copy-start.5 = (s32[1,128]{1,0:T(1,128)S(1)}, s32[1,128]{1,0:T(1,128)}, u32[]{:S(2)}) copy-start(s32[1,128]{1,0:T(1,128)} %constant.4.clone.lanes_ref) | copy-start | bytes 1540
  8.1 3.9 %copy-start = (bf16[4,256,256]{2,1,0:T(8,128)(2,1)S(1)}, bf16[4,256,256]{2,1,0:T(8,128)(2,1)}, u32[]{:S(2)}) copy-start(bf16[4,256,256]{2,1,0:T(8,128)(2,1)} %img_ref.3) | copy-start | bytes 1572868
  8.1 3.9 %copy-start.1 = (f32[2,128,128]{2,1,0:T(8,128)S(1)}, f32[2,128,128]{2,1,0:T(8,128)}, u32[]{:S(2)}) copy-start(f32[2,128,128]{2,1,0:T(8,128)} %fld_ref.3) | copy-start | bytes 393220

commit v6 on v5

--- a/solution.py
+++ b/solution.py
@@ -201,6 +201,8 @@
                     column = 2 * xh + pixel
                     lines = slice(PAD, PAD + span)
                     t_ref[k, 4 + column, parity, side, half, lines, :] = turned(0)
+                    if isinstance(k, int) and k == sections:
+                        continue
                     n = 2 * side + half
                     step, edge, border = (1, 0, column - 4) if xh >= 2 else (-1, per - 1, 12 + column)
                     moved = turned(step)

time: 37.3 us -> 37.3 us (level)
  no operation moved by 1% of the time
where the time goes in v6:
time: 37.3 us; the launch traced here: 37.1 us
  Pallas kernels  28.3 us (76%)
  starting transfers between devices  5.63 us (15%)
  waiting for transfers between devices  2.23 us (6%)
  local copies, waits for them, and re-layouts  0.79 us (2%)
    pallas_call x1, Pallas kernels, on_device(): pl.pallas_call(functools.partial(kernel, sections, rows, rows * count, ch...  25.1 us
    ppermute x1, starting transfers between devices, on_device(): lo = lax.ppermute(up, 'tile', forward)  3.71 us
    ppermute x1, waiting for transfers between devices, on_device(): hi = lax.ppermute(down, 'tile', backward)  2.23 us
    ppermute x1, starting transfers between devices, on_device(): hi = lax.ppermute(down, 'tile', backward)  1.92 us
    pallas_call x1, Pallas kernels, on_device(): pl.pallas_call(prepare, out_shape=(jax.ShapeDtypeStruct((WINDOWS, WIDE, W...  1.65 us
    pallas_call x1, Pallas kernels, on_device(): pl.pallas_call(pack, out_shape=(jax.ShapeDtypeStruct((held, columns), ima...  1.6 us
    unnamed x17, local copies, waits for them, and re-layouts  0.79 us
  transfers between devices with their start and end apart: 2, of which 1 were waited for; matrix products, arithmetic and copies ran while one was open for 0% of the time, Pallas kernels for 4%

profile of v6, /device:TPU:21, one launch (start us, length us, event | category | flops | bytes accessed | tf_op | source)
XLA Modules:
  0.0 37.1 jit_solution(5515783018846404900)
XLA Ops:
  0.0 0.0 copy-start.2
  0.0 0.0 copy-start.7
  0.0 1.6 %pack.1 = (bf16[120,256]{1,0:T(8,128)(2,1)}, bf16[120,256]{1,0:T(8,128)(2,1)}) custom-call(bf16[4,256,256]{2,1,0:T(8,128)(2,1)} %img_ref.3, f32[2,128,128]{2,1,0:T(8,128)} %fld_ref.3), custom_call_target="tpu_custom_call" | custom-call | tf_op jit(solution)/shard_map/pack/pallas_call | solution.py:429
  1.6 0.0 copy-start.6
  1.6 3.7 %collective-permute-start = (bf16[120,256]{1,0:T(8,128)(2,1)}, bf16[120,256]{1,0:T(8,128)(2,1)S(1)}, u32[]{:S(2)}, u32[]{:S(2)}) collective-permute-start(bf16[120,256]{1,0:T(8,128)(2,1)} %get-tuple-element.10), channel_id=1, source_target_pairs={{0,1},{1,2},{2,3},{3,4},{4,5},{5,6},{6,7},{7,8},{8,9},{9,10},{10,1... | collective-permute-start | bytes 184328 | tf_op jit(solution)/shard_map/ppermute | solution.py:442
  5.3 1.9 %collective-permute-start.1 = (bf16[120,256]{1,0:T(8,128)(2,1)}, bf16[120,256]{1,0:T(8,128)(2,1)S(1)}, u32[]{:S(2)}, u32[]{:S(2)}) collective-permute-start(bf16[120,256]{1,0:T(8,128)(2,1)} %get-tuple-element.11), channel_id=1, source_target_pairs={{1,0},{2,1},{3,2},{4,3},{5,4},{6,5},{7,6},{8,7},{9,8},{10,9},{11,1... | collective-permute-start | bytes 184328 | tf_op jit(solution)/shard_map/ppermute | solution.py:443
  7.3 0.0 copy-done.7
  7.3 0.0 copy-done.6
  7.3 0.1 copy.9.c1_ref
  7.4 0.0 copy-start.3
  7.4 0.0 copy-start.4
  7.4 0.0 copy-start.5
  7.4 0.0 copy-done.2
  7.4 0.6 %copy-done.3 = f32[32]{0:T(128)S(1)} copy-done((f32[32]{0:T(128)S(1)}, f32[32]{0:T(128)}, u32[]{:S(2)}) %copy-start.3) | copy-done | bytes 152
  8.1 0.0 copy-done.4
  8.1 0.0 copy-done.5
  8.1 0.0 copy-start
  8.1 0.0 copy-start.1
  8.1 1.7 %weights.1 = (bf16[8,256,256]{2,1,0:T(8,128)(2,1)S(1)}, bf16[4,256,256]{2,1,0:T(8,128)(2,1)S(1)}, f32[8,128]{1,0:T(8,128)S(1)}) custom-call(s32[3]{0:T(128)S(1)} %broadcast_add_fusion.chain_ref, s32[1,128]{1,0:T(1,128)S(1)} %copy-done.5, bf16[32,9]{1,0:T(8,128)(2,1)S(1)} %copy.9.c1_ref, f32[1,32]{1,0:T(1,128)S(1)} %bitcast.2, ...), custom_call_target="tpu_custom_call" | custom-call | flops 1000000000 | bytes 1000000 | tf_op jit(solution)/shard_map/weights/pallas_call | solution.py:445
  9.8 0.0 collective-permute-done.lo_ref
  9.8 2.2 %collective-permute-done.1.hi_ref = bf16[120,256]{1,0:T(8,128)(2,1)S(1)} collective-permute-done((bf16[120,256]{1,0:T(8,128)(2,1)}, bf16[120,256]{1,0:T(8,128)(2,1)S(1)}, u32[]{:S(2)}, u32[]{:S(2)}) %collective-permute-start.1) | collective-permute-done | bytes 61472 | tf_op jit(solution)/shard_map/ppermute | solution.py:443
  12.0 0.0 copy-done
  12.0 0.0 copy-done.1
  12.0 25.1 %align.1 = f32[3,2,128,128]{3,2,1,0:T(8,128)} custom-call(s32[3]{0:T(128)S(1)} %broadcast_add_fusion.chain_ref, bf16[4,256,256]{2,1,0:T(8,128)(2,1)S(1)} %copy-done, bf16[120,256]{1,0:T(8,128)(2,1)S(1)} %collective-permute-done.lo_ref, bf16[120,256]{1,0:T(8,128)(2,1)S(1)} %collective-permute-done.1.hi_ref, f32[2,128,128]{2,1,0:T(8,128)S(1)} %copy-done.1, ...), custom_call_target="tpu_custom_call" | custom-call | tf_op jit(solution)/shard_map/align/pallas_call | solution.py:461
  (1 shorter events, 0.0 us)
Async XLA Ops:
  0.0 7.4 %copy-start.2 = (bf16[9,32,32]{2,1,0:T(8,128)(2,1)S(1)}, bf16[9,32,32]{2,1,0:T(8,128)(2,1)}, u32[]{:S(2)}) copy-start(bf16[9,32,32]{2,1,0:T(8,128)(2,1)} %c2_ref.1) | copy-start | bytes 55300
  0.0 7.3 %copy-start.7 = (s32[3]{0:T(128)S(1)}, s32[3]{0:T(128)}, u32[]{:S(2)}) copy-start(s32[3]{0:T(128)} %param.9) | copy-start | bytes 40
  1.6 5.7 %copy-start.6 = (bf16[32,9]{0,1:T(8,128)(2,1)S(1)}, bf16[32,9]{0,1:T(8,128)(2,1)}, u32[]{:S(2)}) copy-start(bf16[32,9]{0,1:T(8,128)(2,1)} %param.11) | copy-start | bytes 1732
  1.6 8.1 %collective-permute-start = (bf16[120,256]{1,0:T(8,128)(2,1)}, bf16[120,256]{1,0:T(8,128)(2,1)S(1)}, u32[]{:S(2)}, u32[]{:S(2)}) collective-permute-start(bf16[120,256]{1,0:T(8,128)(2,1)} %get-tuple-element.10), channel_id=1, source_target_pairs={{0,1},{1,2},{2,3},{3,4},{4,5},{5,6},{6,7},{7,8},{8,9},{9,10},{10,1... | collective-permute-start | bytes 184328 | tf_op jit(solution)/shard_map/ppermute | solution.py:442
  5.3 6.6 %collective-permute-start.1 = (bf16[120,256]{1,0:T(8,128)(2,1)}, bf16[120,256]{1,0:T(8,128)(2,1)S(1)}, u32[]{:S(2)}, u32[]{:S(2)}) collective-permute-start(bf16[120,256]{1,0:T(8,128)(2,1)} %get-tuple-element.11), channel_id=1, source_target_pairs={{1,0},{2,1},{3,2},{4,3},{5,4},{6,5},{7,6},{8,7},{9,8},{10,9},{11,1... | collective-permute-start | bytes 184328 | tf_op jit(solution)/shard_map/ppermute | solution.py:443
  7.4 0.7 %copy-start.3 = (f32[32]{0:T(128)S(1)}, f32[32]{0:T(128)}, u32[]{:S(2)}) copy-start(f32[32]{0:T(128)} %param.12) | copy-start | bytes 388
  7.4 0.7 %copy-start.4 = (f32[32]{0:T(128)S(1)}, f32[32]{0:T(128)}, u32[]{:S(2)}) copy-start(f32[32]{0:T(128)} %param.14) | copy-start | bytes 388
  7.4 0.7 %copy-start.5 = (s32[1,128]{1,0:T(1,128)S(1)}, s32[1,128]{1,0:T(1,128)}, u32[]{:S(2)}) copy-start(s32[1,128]{1,0:T(1,128)} %constant.4.clone.lanes_ref) | copy-start | bytes 1540
  8.1 3.9 %copy-start = (bf16[4,256,256]{2,1,0:T(8,128)(2,1)S(1)}, bf16[4,256,256]{2,1,0:T(8,128)(2,1)}, u32[]{:S(2)}) copy-start(bf16[4,256,256]{2,1,0:T(8,128)(2,1)} %img_ref.3) | copy-start | bytes 1572868
  8.1 3.9 %copy-start.1 = (f32[2,128,128]{2,1,0:T(8,128)S(1)}, f32[2,128,128]{2,1,0:T(8,128)}, u32[]{:S(2)}) copy-start(f32[2,128,128]{2,1,0:T(8,128)} %fld_ref.3) | copy-start | bytes 393220

commit v7 on v6

--- a/solution.py
+++ b/solution.py
@@ -273,7 +273,6 @@
     lax.fori_loop(0, half, functools.partial(encode, largest, largest), 0)
     encode(fewer, largest, half, 0)
     lax.fori_loop(half + 1, sections + 1, functools.partial(encode, fewer, fewer), 0)
-    features(sections, 3, (a1_ref, b1_ref), fewer)
 
     scale = SHARPNESS / channels * math.log2(math.e)
     sub8 = lax.broadcasted_iota(jnp.int32, (8, LANES), 0)
@@ -406,6 +405,7 @@
 
     for at in range(4):
         fill(0, s0_ref, at // 2, at % 2)
+    features(sections, 3, (a1_ref, b1_ref), fewer)
     turns = pl.cdiv(blocks, 2)
     found = lax.fori_loop(0, turns, two_steps, (jnp.zeros((8, LANES), jnp.float32),) * 4)
     finish(2 * turns - 1, found)

time: 37.3 us -> 37.3 us (level)
  no operation moved by 1% of the time
where the time goes in v7:
time: 37.3 us; the launch traced here: 37.1 us
  Pallas kernels  28.3 us (76%)
  starting transfers between devices  5.63 us (15%)
  waiting for transfers between devices  2.23 us (6%)
  local copies, waits for them, and re-layouts  0.79 us (2%)
    pallas_call x1, Pallas kernels, on_device(): pl.pallas_call(functools.partial(kernel, sections, rows, rows * count, ch...  25.1 us
    ppermute x1, starting transfers between devices, on_device(): lo = lax.ppermute(up, 'tile', forward)  3.71 us
    ppermute x1, waiting for transfers between devices, on_device(): hi = lax.ppermute(down, 'tile', backward)  2.23 us
    ppermute x1, starting transfers between devices, on_device(): hi = lax.ppermute(down, 'tile', backward)  1.92 us
    pallas_call x1, Pallas kernels, on_device(): pl.pallas_call(prepare, out_shape=(jax.ShapeDtypeStruct((WINDOWS, WIDE, W...  1.65 us
    pallas_call x1, Pallas kernels, on_device(): pl.pallas_call(pack, out_shape=(jax.ShapeDtypeStruct((held, columns), ima...  1.6 us
    unnamed x17, local copies, waits for them, and re-layouts  0.79 us
  transfers between devices with their start and end apart: 2, of which 1 were waited for; matrix products, arithmetic and copies ran while one was open for 0% of the time, Pallas kernels for 4%

profile of v7, /device:TPU:21, one launch (start us, length us, event | category | flops | bytes accessed | tf_op | source)
XLA Modules:
  0.0 37.1 jit_solution(5515783018846404900)
XLA Ops:
  0.0 0.0 copy-start.2
  0.0 0.0 copy-start.7
  0.0 1.6 %pack.1 = (bf16[120,256]{1,0:T(8,128)(2,1)}, bf16[120,256]{1,0:T(8,128)(2,1)}) custom-call(bf16[4,256,256]{2,1,0:T(8,128)(2,1)} %img_ref.3, f32[2,128,128]{2,1,0:T(8,128)} %fld_ref.3), custom_call_target="tpu_custom_call" | custom-call | tf_op jit(solution)/shard_map/pack/pallas_call | solution.py:429
  1.6 0.0 copy-start.6
  1.6 3.7 %collective-permute-start = (bf16[120,256]{1,0:T(8,128)(2,1)}, bf16[120,256]{1,0:T(8,128)(2,1)S(1)}, u32[]{:S(2)}, u32[]{:S(2)}) collective-permute-start(bf16[120,256]{1,0:T(8,128)(2,1)} %get-tuple-element.10), channel_id=1, source_target_pairs={{0,1},{1,2},{2,3},{3,4},{4,5},{5,6},{6,7},{7,8},{8,9},{9,10},{10,1... | collective-permute-start | bytes 184328 | tf_op jit(solution)/shard_map/ppermute | solution.py:442
  5.3 1.9 %collective-permute-start.1 = (bf16[120,256]{1,0:T(8,128)(2,1)}, bf16[120,256]{1,0:T(8,128)(2,1)S(1)}, u32[]{:S(2)}, u32[]{:S(2)}) collective-permute-start(bf16[120,256]{1,0:T(8,128)(2,1)} %get-tuple-element.11), channel_id=1, source_target_pairs={{1,0},{2,1},{3,2},{4,3},{5,4},{6,5},{7,6},{8,7},{9,8},{10,9},{11,1... | collective-permute-start | bytes 184328 | tf_op jit(solution)/shard_map/ppermute | solution.py:443
  7.3 0.0 copy-done.7
  7.3 0.0 copy-done.6
  7.3 0.1 copy.9.c1_ref
  7.4 0.0 copy-start.3
  7.4 0.0 copy-start.4
  7.4 0.0 copy-start.5
  7.4 0.0 copy-done.2
  7.4 0.6 %copy-done.3 = f32[32]{0:T(128)S(1)} copy-done((f32[32]{0:T(128)S(1)}, f32[32]{0:T(128)}, u32[]{:S(2)}) %copy-start.3) | copy-done | bytes 152
  8.1 0.0 copy-done.4
  8.1 0.0 copy-done.5
  8.1 0.0 copy-start
  8.1 0.0 copy-start.1
  8.1 1.7 %weights.1 = (bf16[8,256,256]{2,1,0:T(8,128)(2,1)S(1)}, bf16[4,256,256]{2,1,0:T(8,128)(2,1)S(1)}, f32[8,128]{1,0:T(8,128)S(1)}) custom-call(s32[3]{0:T(128)S(1)} %broadcast_add_fusion.chain_ref, s32[1,128]{1,0:T(1,128)S(1)} %copy-done.5, bf16[32,9]{1,0:T(8,128)(2,1)S(1)} %copy.9.c1_ref, f32[1,32]{1,0:T(1,128)S(1)} %bitcast.2, ...), custom_call_target="tpu_custom_call" | custom-call | flops 1000000000 | bytes 1000000 | tf_op jit(solution)/shard_map/weights/pallas_call | solution.py:445
  9.8 0.0 collective-permute-done.lo_ref
  9.8 2.2 %collective-permute-done.1.hi_ref = bf16[120,256]{1,0:T(8,128)(2,1)S(1)} collective-permute-done((bf16[120,256]{1,0:T(8,128)(2,1)}, bf16[120,256]{1,0:T(8,128)(2,1)S(1)}, u32[]{:S(2)}, u32[]{:S(2)}) %collective-permute-start.1) | collective-permute-done | bytes 61472 | tf_op jit(solution)/shard_map/ppermute | solution.py:443
  12.0 0.0 copy-done
  12.0 0.0 copy-done.1
  12.0 25.1 %align.1 = f32[3,2,128,128]{3,2,1,0:T(8,128)} custom-call(s32[3]{0:T(128)S(1)} %broadcast_add_fusion.chain_ref, bf16[4,256,256]{2,1,0:T(8,128)(2,1)S(1)} %copy-done, bf16[120,256]{1,0:T(8,128)(2,1)S(1)} %collective-permute-done.lo_ref, bf16[120,256]{1,0:T(8,128)(2,1)S(1)} %collective-permute-done.1.hi_ref, f32[2,128,128]{2,1,0:T(8,128)S(1)} %copy-done.1, ...), custom_call_target="tpu_custom_call" | custom-call | tf_op jit(solution)/shard_map/align/pallas_call | solution.py:461
  (1 shorter events, 0.0 us)
Async XLA Ops:
  0.0 7.4 %copy-start.2 = (bf16[9,32,32]{2,1,0:T(8,128)(2,1)S(1)}, bf16[9,32,32]{2,1,0:T(8,128)(2,1)}, u32[]{:S(2)}) copy-start(bf16[9,32,32]{2,1,0:T(8,128)(2,1)} %c2_ref.1) | copy-start | bytes 55300
  0.0 7.3 %copy-start.7 = (s32[3]{0:T(128)S(1)}, s32[3]{0:T(128)}, u32[]{:S(2)}) copy-start(s32[3]{0:T(128)} %param.9) | copy-start | bytes 40
  1.6 5.7 %copy-start.6 = (bf16[32,9]{0,1:T(8,128)(2,1)S(1)}, bf16[32,9]{0,1:T(8,128)(2,1)}, u32[]{:S(2)}) copy-start(bf16[32,9]{0,1:T(8,128)(2,1)} %param.11) | copy-start | bytes 1732
  1.6 8.1 %collective-permute-start = (bf16[120,256]{1,0:T(8,128)(2,1)}, bf16[120,256]{1,0:T(8,128)(2,1)S(1)}, u32[]{:S(2)}, u32[]{:S(2)}) collective-permute-start(bf16[120,256]{1,0:T(8,128)(2,1)} %get-tuple-element.10), channel_id=1, source_target_pairs={{0,1},{1,2},{2,3},{3,4},{4,5},{5,6},{6,7},{7,8},{8,9},{9,10},{10,1... | collective-permute-start | bytes 184328 | tf_op jit(solution)/shard_map/ppermute | solution.py:442
  5.3 6.6 %collective-permute-start.1 = (bf16[120,256]{1,0:T(8,128)(2,1)}, bf16[120,256]{1,0:T(8,128)(2,1)S(1)}, u32[]{:S(2)}, u32[]{:S(2)}) collective-permute-start(bf16[120,256]{1,0:T(8,128)(2,1)} %get-tuple-element.11), channel_id=1, source_target_pairs={{1,0},{2,1},{3,2},{4,3},{5,4},{6,5},{7,6},{8,7},{9,8},{10,9},{11,1... | collective-permute-start | bytes 184328 | tf_op jit(solution)/shard_map/ppermute | solution.py:443
  7.4 0.7 %copy-start.3 = (f32[32]{0:T(128)S(1)}, f32[32]{0:T(128)}, u32[]{:S(2)}) copy-start(f32[32]{0:T(128)} %param.12) | copy-start | bytes 388
  7.4 0.7 %copy-start.4 = (f32[32]{0:T(128)S(1)}, f32[32]{0:T(128)}, u32[]{:S(2)}) copy-start(f32[32]{0:T(128)} %param.14) | copy-start | bytes 388
  7.4 0.7 %copy-start.5 = (s32[1,128]{1,0:T(1,128)S(1)}, s32[1,128]{1,0:T(1,128)}, u32[]{:S(2)}) copy-start(s32[1,128]{1,0:T(1,128)} %constant.4.clone.lanes_ref) | copy-start | bytes 1540
  8.1 3.9 %copy-start = (bf16[4,256,256]{2,1,0:T(8,128)(2,1)S(1)}, bf16[4,256,256]{2,1,0:T(8,128)(2,1)}, u32[]{:S(2)}) copy-start(bf16[4,256,256]{2,1,0:T(8,128)(2,1)} %img_ref.3) | copy-start | bytes 1572868
  8.1 3.9 %copy-start.1 = (f32[2,128,128]{2,1,0:T(8,128)S(1)}, f32[2,128,128]{2,1,0:T(8,128)}, u32[]{:S(2)}) copy-start(f32[2,128,128]{2,1,0:T(8,128)} %fld_ref.3) | copy-start | bytes 393220
